TPU v7x, 1024 devices: a whole 4x8x16 slice. The times are simulated.
1024 devices in a mesh: pipe: 16 (over y, core), ctx: 64 (over z, x).
Axes of the slice: x: 4, y: 8, z: 16, core: 2. Of those that a mesh axis runs over, the one named last changes fastest.
Arguments:
- incoming: bfloat16 [16, 8192, 1024], P('pipe', 'ctx'), may hold values from -6 to 6
- fresh: bfloat16 [8192, 1024], P('ctx'), may hold values from -6 to 6
- w_uvqk: bfloat16 [16, 1024, 2048], P('pipe'), may hold values from -0.1875 to 0.1875
- w_out: bfloat16 [16, 512, 1024], P('pipe'), may hold values from -0.25 to 0.25
- cache_kv: bfloat16 [16, 2, 1024, 1024], P('pipe', None, 'ctx'), may hold values from -6 to 6
- rows_user: int32 [17, 8192], P(None, 'ctx'), may hold values from 0 to 3, never falling along the last dimension, each value on 1 to 4096 neighbouring positions
- cache_len: int32 [17, 4], replicated, may hold values from 1 to 512, 1024 in all within a row
Outputs:
- section_out: bfloat16 [16, 2, 8192, 1024], P('pipe', None, 'ctx')
Inputs may be any that keep to these rules, and one draw needn't show every extreme that they name: `rows_user`: each micro-batch's row users never fall along the events; every user has at least one event. `cache_len`: each micro-batch's row sums to 1024.
All inputs are finite; a program needn't handle non-finite values.
Results may differ from a plain program's by a relative error of at most 0.0085.
Values may be sent and summed in bfloat16 or wider, within the bound.
No kernel may reach another device: no remote copies, remote signals or barrier semaphores. Data moves between devices by JAX's collectives and lax.ppermute only.
A program may use at most 32 MiB of HBM per device.

v0:
```python
import math

import jax
import jax.numpy as jnp
from jax import lax
from jax.sharding import PartitionSpec as P

HEADS = 4
STEPS = 2


def passed_along(block, axis, distance):
    devices = range(lax.axis_size(axis))
    route = [(i - distance, i) for i in devices if i - distance in devices]
    return lax.ppermute(block, axis, route)


def normalize(values):
    center = jnp.mean(values, axis=-1, keepdims=True)
    shifted = values - center
    spread = jnp.mean(shifted * shifted, axis=-1, keepdims=True)
    return shifted * lax.rsqrt(spread + 1e-06)


def owners(positions, lengths):
    bounds = jnp.cumsum(lengths)
    return jnp.sum((positions[:, None] >= bounds[None, :-1]).astype(jnp.int32), axis=1)


def attend(queries, kv_rows, allowed):
    width = kv_rows.shape[1] // 2
    count = kv_rows.shape[0]
    key_part = kv_rows[:, :width].reshape(count, HEADS, -1)
    value_part = kv_rows[:, width:].reshape(count, HEADS, -1)
    scale = queries.shape[2] ** (-0.5)
    scores = jnp.einsum("thd,nhd->htn", queries, key_part, preferred_element_type=jnp.float32)
    weights = (jax.nn.silu(scale * scores) * allowed[None].astype(jnp.float32)).astype(jnp.bfloat16)
    summed = jnp.einsum("htn,nhd->thd", weights, value_part, preferred_element_type=jnp.float32)
    return summed.reshape(queries.shape[0], width)


def cache_blocks(attn, all_rows, queries, users, lengths):
    block_rows = math.gcd(all_rows.shape[0], 128)
    blocks = all_rows.reshape(-1, block_rows, all_rows.shape[1])

    def scan_body(total, packed):
        order, segment = packed
        positions = order * block_rows + jnp.arange(block_rows, dtype=jnp.int32)
        allowed = users[:, None] == owners(positions, lengths)[None, :]
        addition = attend(queries, segment, allowed)
        return (total + addition, None)

    result, unused = lax.scan(
        scan_body, attn, (jnp.arange(blocks.shape[0], dtype=jnp.int32), blocks)
    )
    return result


def body(incoming, fresh, w_uvqk, w_out, cache_kv, rows_user, cache_len):
    section = lax.axis_index("pipe")
    sections = lax.axis_size("pipe")
    local_rows = fresh.shape[0]
    width = w_out.shape[1]
    weights_in = w_uvqk[0]
    weights_back = w_out[0]
    row_index = jnp.arange(local_rows, dtype=jnp.int32)
    causal = row_index[None, :] <= row_index[:, None]
    results = []
    current = incoming[0]
    for step_index in range(STEPS):
        if step_index > 0:
            passed = passed_along(results[-1], "pipe", 1)
            current = jnp.where(section == 0, fresh, passed)
        batch_index = sections - 1 - section + step_index
        users = lax.dynamic_index_in_dim(rows_user, batch_index, 0, keepdims=False)
        lengths = lax.dynamic_index_in_dim(cache_len, batch_index, 0, keepdims=False)
        normed = normalize(current.astype(jnp.float32)).astype(jnp.bfloat16)
        projected = jax.nn.silu(
            jnp.dot(normed, weights_in, preferred_element_type=jnp.float32)
        ).astype(jnp.bfloat16)
        gate_u = projected[:, :width]
        queries = projected[:, width : 2 * width].reshape(local_rows, HEADS, -1)
        same_user = users[:, None] == users[None, :]
        attn = attend(queries, projected[:, 2 * width :], causal & same_user)
        all_rows = lax.all_gather(cache_kv[0, step_index], "ctx", axis=0, tiled=True)
        attn = cache_blocks(attn, all_rows, queries, users, lengths)
        mixed = (normalize(attn) * gate_u.astype(jnp.float32)).astype(jnp.bfloat16)
        result = (
            jnp.dot(mixed, weights_back, preferred_element_type=jnp.float32)
            + current.astype(jnp.float32)
        ).astype(jnp.bfloat16)
        results.append(result)
    return jnp.stack(results)[None]


def solution(mesh):
    in_specs = (
        P("pipe", "ctx", None),
        P("ctx", None),
        P("pipe", None, None),
        P("pipe", None, None),
        P("pipe", None, "ctx", None),
        P(None, "ctx"),
        P(),
    )
    out_specs = P("pipe", None, "ctx", None)
    return jax.shard_map(body, mesh=mesh, in_specs=in_specs, out_specs=out_specs, check_vma=False)
```

profile of v0, /device:TPU:8, one launch (start us, length us, event | category | flops | bytes accessed | tf_op | source)
XLA Modules:
  0.0 348.1 jit_solution(7326069109381252536)
XLA Ops:
  6.5 1.5 fusion.77
  8.8 1.1 convert_reduce_fusion.3
  9.9 1.2 fusion.33
  11.1 3.1 multiply_convert_fusion.3
  16.1 151.3 %all-gather.5.cloned.1.call-done = bf16[1,1,1024,1024]{3,2,1,0:T(8,128)(2,1)} async-done(((bf16[1,1,16,1024]{3,2,1,0:T(8,128)(2,1)}), bf16[1,1,1024,1024]{3,2,1,0:T(8,128)(2,1)}) %all-gather.5.cloned.1.call-update) | async-done | bytes 2097168 | tf_op jit(solution)/shard_map/all_gather | solution.py:85
  167.4 24.7 %while.24 = (s32[]{:T(128)}, f32[128,512]{0,1:T(8,128)S(1)}, bf16[8,128,1024]{2,1,0:T(8,128)(2,1)}, bf16[128,4,128]{2,0,1:T(8,128)(2,1)S(1)}, s32[128]{0:T(128)S...) while((s32[]{:T(128)}, f32[128,512]{0,1:T(8,128)S(1)}, ...), condition=%wide.region_5.6_spmd, body=%wide.region_3.5_spmd.sunk | while | flops 34112640 | bytes 3148457 | solution.py:53
  167.4 1.0 constant_dynamic-slice_fusion.6
  170.6 1.0 constant_dynamic-slice_fusion.6
  173.6 1.0 constant_dynamic-slice_fusion.6
  176.7 1.0 constant_dynamic-slice_fusion.6
  179.8 1.0 constant_dynamic-slice_fusion.6
  182.9 1.0 constant_dynamic-slice_fusion.6
  186.0 1.0 constant_dynamic-slice_fusion.6
  193.0 1.9 collective-permute-start
  195.1 5.6 %collective-permute-done = bf16[128,1024]{1,0:T(8,128)(2,1)S(1)} collective-permute-done((bf16[128,1024]{1,0:T(8,128)(2,1)S(1)}, bf16[128,1024]{1,0:T(8,128)(2,1)S(1)}, u32[]{:S(2)}, u32[]{:S(2)}) %collective-permute-start) | collective-permute-done | bytes 262176 | tf_op jit(solution)/shard_map/ppermute | solution.py:15
  201.0 3.0 multiply_convert_fusion.2
  204.7 110.0 %all-gather.7.cloned.1.call-done = bf16[1,1,1024,1024]{3,2,1,0:T(8,128)(2,1)} async-done(((bf16[1,1,16,1024]{3,2,1,0:T(8,128)(2,1)}), bf16[1,1,1024,1024]{3,2,1,0:T(8,128)(2,1)}) %all-gather.7.cloned.1.call-update) | async-done | bytes 2097168 | tf_op jit(solution)/shard_map/all_gather | solution.py:85
  314.7 24.9 %while.25 = (s32[]{:T(128)}, f32[128,512]{0,1:T(8,128)S(1)}, bf16[8,128,1024]{2,1,0:T(8,128)(2,1)}, bf16[128,4,128]{2,0,1:T(8,128)(2,1)S(1)}, s32[128]{0:T(128)S...) while((s32[]{:T(128)}, f32[128,512]{0,1:T(8,128)S(1)}, ...), condition=%wide.region_13.14_spmd, body=%wide.region_11.13_spmd.sunk | while | flops 34112640 | bytes 3148457 | solution.py:53
  317.9 1.0 constant_dynamic-slice_fusion.7
  321.0 1.0 constant_dynamic-slice_fusion.7
  324.1 1.0 constant_dynamic-slice_fusion.7
  327.2 1.0 constant_dynamic-slice_fusion.7
  330.3 1.0 constant_dynamic-slice_fusion.7
  333.4 1.0 constant_dynamic-slice_fusion.7
  (193 shorter events, 31.8 us)
Async XLA Ops:
  6.5 186.0 %copy-start = (bf16[1,512,1024]{2,1,0:T(8,128)(2,1)S(1)}, bf16[1,512,1024]{2,1,0:T(8,128)(2,1)}, u32[]{:S(2)}) copy-start(bf16[1,512,1024]{2,1,0:T(8,128)(2,1)} %param.14) | copy-start | bytes 3145732
  6.5 160.9 %all-gather.5.cloned.1.call-start = ((), (), s32[]{:S(2)}) async-start(), calls=%async_computation | async-start | bytes 2129920 | tf_op jit(solution)/shard_map/all_gather | solution.py:85
  8.0 306.7 %all-gather.7.cloned.1.call-start = ((), (), s32[]{:S(2)}) async-start(), calls=%async_computation.1 | async-start | bytes 2129920 | tf_op jit(solution)/shard_map/all_gather | solution.py:85
  11.1 4.1 %copy-start.3 = (s32[17,4]{0,1:T(4,128)S(1)}, s32[17,4]{0,1:T(4,128)}, u32[]{:S(2)}) copy-start(s32[17,4]{0,1:T(4,128)} %param.17) | copy-start | bytes 820
  167.4 25.2 %copy-start.1 = (bf16[1,128,1024]{2,1,0:T(8,128)(2,1)S(1)}, bf16[1,128,1024]{2,1,0:T(8,128)(2,1)}, u32[]{:S(2)}) copy-start(bf16[1,128,1024]{2,1,0:T(8,128)(2,1)} %param.11) | copy-start | bytes 786436
  167.4 33.2 %copy-start.2 = (bf16[128,1024]{1,0:T(8,128)(2,1)S(1)}, bf16[128,1024]{1,0:T(8,128)(2,1)}, u32[]{:S(2)}) copy-start(bf16[128,1024]{1,0:T(8,128)(2,1)} %param.12) | copy-start | bytes 786436
  193.0 7.7 %collective-permute-start = (bf16[128,1024]{1,0:T(8,128)(2,1)S(1)}, bf16[128,1024]{1,0:T(8,128)(2,1)S(1)}, u32[]{:S(2)}, u32[]{:S(2)}) collective-permute-start(bf16[128,1024]{1,0:T(8,128)(2,1)S(1)} %fusion.18), channel_id=1, source_target_pairs={{0,64},{64,128},{128,192},{192,256},{256,320},{320,384},{384,448},... | collective-permute-start | bytes 786440 | tf_op jit(solution)/shard_map/ppermute | solution.py:15
Sparse Core Ops, SparseCore 0:
  11.4 155.9 all-gather.4
  171.5 143.1 all-gather.6
where the time goes:
time: 349 us; the launch traced here: 348 us
  waiting for transfers between devices  268 us (77%)
  local copies, waits for them, and re-layouts  31.3 us (9%)
  matrix products  14.4 us (4%)
  between operations  13.6 us (4%)
  loops' own time  11.3 us (3%)
  other arithmetic  7.94 us (2%)
    all_gather x2, waiting for transfers between devices, body(): lax.all_gather(cache_kv[0, step_index], 'ctx', axis=0, tiled=True)  261 us
    dynamic_slice x48, local copies, waits for them, and re-layouts, cache_blocks(): lax.scan(scan_body, attn, (jnp.arange(blocks.shape[0], dtype=jnp.int32),...  27.8 us
    another operation x2, loops' own time, cache_blocks(): lax.scan(scan_body, attn, (jnp.arange(blocks.shape[0], dtype=jnp.int32),...  11.3 us
    dot_general x18, matrix products, attend(): jnp.einsum('htn,nhd->thd', weights, value_part, preferred_element_type=jn...  7.44 us
  transfers between devices with their start and end apart: 3, of which 3 were waited for; matrix products, arithmetic and copies ran while one was open for 9% of the time, Pallas kernels for 0%

commit v1 on v0

v1 whole, which is shorter than its diff:
```python
import functools

import jax
import jax.numpy as jnp
from jax import lax
from jax.experimental import pallas as pl
from jax.experimental.pallas import tpu as pltpu
from jax.sharding import PartitionSpec as P


HEADS = 4
HD = 128
HW = HEADS * HD
STEPS = 2
NX = 4
NZ = 16
USERS = 4
SHARE = 16
EVENS = [[z * NX + x for z in range(p, NZ, 2)] for p in range(2) for x in range(NX)]
SQUARES = [[(2 * i + p) * NX + x for p in range(2) for x in range(NX)] for i in range(NZ // 2)]
PAIR = [(c, (c // NX ^ 1) * NX + c % NX) for c in range(NX * NZ)]
SPAN = SHARE * NZ // 2


def along_x(distance):
    return [(c, (c // NX) * NX + (c % NX + distance) % NX) for c in range(NX * NZ)]


def half_silu(half):
    return half + half * jnp.tanh(half)


def normalize(values):
    center = jnp.mean(values, axis=-1, keepdims=True)
    shifted = values - center
    spread = jnp.mean(shifted * shifted, axis=-1, keepdims=True)
    return shifted * lax.rsqrt(spread + 1e-06)


def dot_t(a, b):
    return lax.dot_general(a, b, (((1,), (1,)), ((), ())), preferred_element_type=jnp.float32)


def user_columns(users_ref, step):
    batch = lax.axis_size("pipe") - 1 - lax.axis_index("pipe") + step
    row = users_ref[pl.ds(batch, 1), :].astype(jnp.float32)
    square = jnp.broadcast_to(row, (row.shape[1], row.shape[1]))
    return square, square.T


def current_of(refs, step):
    if step == 0:
        return refs[0][...]
    passed, fresh = refs
    return jnp.where(lax.axis_index("pipe") == 0, fresh[...], passed[...])


def project_kernel(step, n_x, *refs):
    x_refs, (w_ref, users_ref, uq_ref, attn_ref, normed, keys) = refs[:n_x], refs[n_x:]
    part = pl.program_id(0)

    @pl.when(part == 0)
    def _():
        x = current_of(x_refs, step).astype(jnp.float32)
        normed[...] = normalize(x).astype(jnp.bfloat16)

    def projected():
        wide = jnp.dot(normed[...], w_ref[...], preferred_element_type=jnp.float32)
        return half_silu(0.5 * wide).astype(jnp.bfloat16)

    @pl.when(part == 0)
    def _():
        uq_ref[:, HW:] = projected()

    @pl.when(part == 1)
    def _():
        keys[...] = projected()

    @pl.when(part == 2)
    def _():
        values = projected()
        rows, columns = user_columns(users_ref, step)
        t = lax.broadcasted_iota(jnp.int32, rows.shape, 0)
        n = lax.broadcasted_iota(jnp.int32, rows.shape, 1)
        allowed = (rows == columns) & (n <= t)
        for h in range(HEADS):
            s = slice(h * HD, (h + 1) * HD)
            scores = dot_t(uq_ref[:, HW + h * HD : HW + (h + 1) * HD], keys[:, s])
            weights = jnp.where(allowed, half_silu((0.5 * HD**-0.5) * scores), 0.0)
            attn_ref[:, s] = jnp.dot(
                weights.astype(jnp.bfloat16), values[:, s], preferred_element_type=jnp.float32
            )

    @pl.when(part == 3)
    def _():
        uq_ref[:, :HW] = projected()


def attend_kernel(step, n_x, sizes, *refs):
    count = len(sizes)
    x_refs, refs = refs[:n_x], refs[n_x:]
    u_ref, q_ref, local_ref, w_ref, users_ref, len_ref = refs[:6]
    key_refs, value_refs = refs[6 : 6 + count], refs[6 + count : 6 + 2 * count]
    rest = refs[6 + 2 * count :]
    if step > 0:
        first_ref, out_ref, attn, masks = rest
    else:
        out_ref, attn, masks = rest
    head = pl.program_id(0)
    place = lax.axis_index("ctx")
    x0, z0 = place % NX, place // NX

    @pl.when(head == 0)
    def _():
        batch = lax.axis_size("pipe") - 1 - lax.axis_index("pipe") + step
        bounds, total = [], 0
        for g in range(USERS - 1):
            total = total + len_ref[batch, g]
            bounds.append(total)
        _, columns = user_columns(users_ref, step)
        n = lax.broadcasted_iota(jnp.int32, (8, SPAN), 1)
        base = (n // SHARE) * (2 * NX * SHARE) + n % SHARE
        for b in range(2 * NX):
            if step == 0:
                offset = b * SHARE
            else:
                offset = ((z0 + b) % 2) * (NX * SHARE) + ((x0 + (0, 3, 1, 2)[b // 2]) % NX) * SHARE
            position = base + offset
            owner = sum((position >= bound).astype(jnp.int32) for bound in bounds)
            row = jnp.broadcast_to(owner[:1].astype(jnp.float32), columns.shape)
            masks[:, b * SPAN : (b + 1) * SPAN] = (row == columns).astype(jnp.float32)

    queries = q_ref[...]
    total = local_ref[...]
    at = 0
    for key_ref, value_ref, size in zip(key_refs, value_refs, sizes):
        for begin in range(0, size, 2 * SPAN):
            wide = min(2 * SPAN, size - begin)
            scores = dot_t(queries, key_ref[begin : begin + wide, :])
            weights = half_silu((0.5 * HD**-0.5) * scores) * masks[:, at : at + wide]
            total = total + jnp.dot(
                weights.astype(jnp.bfloat16),
                value_ref[begin : begin + wide, :],
                preferred_element_type=jnp.float32,
            )
            at += wide
    attn[head] = total

    @pl.when(head == HEADS - 1)
    def _():
        whole = jnp.concatenate([attn[h] for h in range(HEADS)], axis=1)
        mixed = (normalize(whole) * u_ref[...].astype(jnp.float32)).astype(jnp.bfloat16)
        result = jnp.dot(mixed, w_ref[...], preferred_element_type=jnp.float32)
        result = (result + current_of(x_refs, step).astype(jnp.float32)).astype(jnp.bfloat16)
        if step > 0:
            out_ref[0] = first_ref[...]
            out_ref[1] = result
        else:
            out_ref[...] = result


def whole(shape):
    return pl.BlockSpec(shape, lambda j: (0,) * len(shape))


def project(step, x_list, w, users):
    t, d = x_list[0].shape
    return pl.pallas_call(
        functools.partial(project_kernel, step, len(x_list)),
        grid=(4,),
        in_specs=[whole((t, d)) for _ in x_list]
        + [pl.BlockSpec((d, HW), lambda j: (0, (j + 1) % 4)), whole(users.shape)],
        out_specs=[whole((t, 2 * HW)), whole((t, HW))],
        out_shape=[
            jax.ShapeDtypeStruct((t, 2 * HW), jnp.bfloat16),
            jax.ShapeDtypeStruct((t, HW), jnp.float32),
        ],
        scratch_shapes=[pltpu.VMEM((t, d), jnp.bfloat16), pltpu.VMEM((t, HW), jnp.bfloat16)],
    )(*x_list, w, users)


def attend(step, x_list, uq, local, w_back, users, lengths, rows, first=None):
    t, d = x_list[0].shape
    sizes = [r.shape[0] for r in rows]
    shape = (t, d) if step == 0 else (STEPS, t, d)
    in_specs = [whole((t, d)) for _ in x_list]
    in_specs += [
        pl.BlockSpec((t, HW), lambda j: (0, 0)),
        pl.BlockSpec((t, HD), lambda j: (0, HEADS + j)),
        pl.BlockSpec((t, HD), lambda j: (0, j)),
        whole((HW, d)),
        whole(users.shape),
        pl.BlockSpec(memory_space=pltpu.SMEM),
    ]
    in_specs += [pl.BlockSpec((size, HD), lambda j: (0, j)) for size in sizes]
    in_specs += [pl.BlockSpec((size, HD), lambda j: (0, HEADS + j)) for size in sizes]
    args = [*x_list, uq, uq, local, w_back, users, lengths, *rows, *rows]
    if step > 0:
        in_specs.append(whole((t, d)))
        args.append(first)
    return pl.pallas_call(
        functools.partial(attend_kernel, step, len(x_list), sizes),
        grid=(HEADS,),
        in_specs=in_specs,
        out_specs=whole(shape),
        out_shape=jax.ShapeDtypeStruct(shape, jnp.bfloat16),
        scratch_shapes=[
            pltpu.VMEM((HEADS, t, HD), jnp.float32),
            pltpu.VMEM((t, sum(sizes)), jnp.float32),
        ],
    )(*args)


def body(incoming, fresh, w_uvqk, w_out, cache_kv, rows_user, cache_len):
    w_in, w_back = w_uvqk[0], w_out[0]
    evens = lax.all_gather(cache_kv[0], "ctx", axis=0, tiled=False, axis_index_groups=EVENS)
    column = [evens[:, t].reshape(SPAN, 2 * HW) for t in range(STEPS)]
    other = lax.ppermute(column[1], "ctx", PAIR)
    spread = jnp.broadcast_to(column[0][None], (2 * NX, SPAN, 2 * HW))
    rows0 = lax.all_to_all(spread, "ctx", 0, 0, axis_index_groups=SQUARES)
    rows0 = rows0.reshape(2 * NX * SPAN, 2 * HW)
    mine, other, rows0 = lax.optimization_barrier((column[1], other, rows0))
    near = jnp.concatenate([mine, other], axis=0)
    from_left = lax.ppermute(near, "ctx", along_x(1))
    from_right = lax.ppermute(near, "ctx", along_x(-1))
    across = lax.ppermute(mine, "ctx", along_x(2))
    across = [across, lax.ppermute(other, "ctx", along_x(-2))]
    rows1 = [near, from_left, from_right, *across]
    uq, local = project(0, [incoming[0]], w_in, rows_user)
    first = attend(0, [incoming[0]], uq, local, w_back, rows_user, cache_len, [rows0])
    sections = lax.axis_size("pipe")
    passed = lax.ppermute(first, "pipe", [(i, i + 1) for i in range(sections - 1)])
    uq, local = project(1, [passed, fresh], w_in, rows_user)
    both = attend(1, [passed, fresh], uq, local, w_back, rows_user, cache_len, rows1, first)
    return both[None]


def solution(mesh):
    in_specs = (
        P("pipe", "ctx", None),
        P("ctx", None),
        P("pipe", None, None),
        P("pipe", None, None),
        P("pipe", None, "ctx", None),
        P(None, "ctx"),
        P(),
    )
    out_specs = P("pipe", None, "ctx", None)
    return jax.shard_map(body, mesh=mesh, in_specs=in_specs, out_specs=out_specs, check_vma=False)
```

time: 349 us -> 122 us (0.35)
  the two profiles are of different devices: /device:TPU:8 before, /device:TPU:1 now
where the time goes in v1:
time: 122 us
  blocking collectives  37.1 us (30%)
  starting transfers between devices  33.8 us (28%)
  waiting for transfers between devices  23.7 us (19%)
  Pallas kernels  22.2 us (18%)
  local copies, waits for them, and re-layouts  4.61 us (4%)
    all_gather x1, blocking collectives, body(): lax.all_gather(cache_kv[0], 'ctx', axis=0, tiled=False, axis_index_groups...  37.1 us
    ppermute x1, waiting for transfers between devices, body(): other = lax.ppermute(column[1], 'ctx', PAIR)  20.6 us
    pallas_call x2, Pallas kernels, attend(): pl.pallas_call(functools.partial(attend_kernel, step, len(x_list), sizes)...  12.1 us
    ppermute x1, starting transfers between devices, body(): lax.ppermute(first, 'pipe', [(i, i + 1) for i in range(sections - 1)])  10.9 us
    pallas_call x2, Pallas kernels, project(): pl.pallas_call(functools.partial(project_kernel, step, len(x_list)), grid...  10.1 us
    all_to_all x1, starting transfers between devices, body(): rows0 = lax.all_to_all(spread, 'ctx', 0, 0, axis_index_groups=SQUARES)  6.1 us
    ppermute x1, starting transfers between devices, body(): from_right = lax.ppermute(near, 'ctx', along_x(-1))  3.62 us
    ppermute x1, starting transfers between devices, body(): across = [across, lax.ppermute(other, 'ctx', along_x(-2))]  3.39 us
  transfers between devices with their start and end apart: 7, of which 2 were waited for; matrix products, arithmetic and copies ran while one was open for 1% of the time, Pallas kernels for 13%

profile of v1, /device:TPU:1, one launch (start us, length us, event | category | flops | bytes accessed | tf_op | source)
XLA Modules:
  0.0 121.6 jit_solution(16190921683001882607)
XLA Ops:
  0.0 37.1 %all_gather.3 = bf16[8,2,16,1024]{3,2,1,0:T(8,128)(2,1)S(1)} all-gather(bf16[1,2,16,1024]{3,2,1,0:T(8,128)(2,1)} %param.11), channel_id=1, replica_groups={{0,8,16,24,32,40,48,56},{1,9,17,25,33,41,49,57},{2,10,18,26,34,42,50,58..., dimensions={0}, use_global_device_ids=true | all-gather | bytes 589824 | tf_op jit(solution)/shard_map/all_gather | solution.py:216
  37.1 1.6 %broadcast_in_dim.11 = bf16[8,128,1024]{2,1,0:T(8,128)(2,1)} broadcast(bf16[128,1024]{1,0:T(8,128)(2,1)S(1)} %bitcast.15), dimensions={1,2} | broadcast | bytes 2359296 | tf_op jit(solution)/shard_map/broadcast_in_dim | solution.py:219
  38.7 6.1 %all-to-all-start = ((bf16[8,128,1024]{2,1,0:T(8,128)(2,1)}), bf16[8,128,1024]{2,1,0:T(8,128)(2,1)S(1)}, u32[]{:S(2)}, u32[]{:S(2)}) async-start(bf16[8,128,1024]{2,1,0:T(8,128)(2,1)} %broadcast_in_dim.11), calls=%async_computation | async-start | bytes 4194304 | tf_op jit(solution)/shard_map/all_to_all | solution.py:220
  44.8 3.4 %collective-permute-start = (bf16[128,1024]{1,0:T(8,128)(2,1)S(1)}, bf16[128,1024]{1,0:T(8,128)(2,1)S(1)}, u32[]{:S(2)}, u32[]{:S(2)}) collective-permute-start(bf16[128,1024]{1,0:T(8,128)(2,1)S(1)} %bitcast.16), channel_id=1, source_target_pairs={{0,4},{1,5},{2,6},{3,7},{4,0},{5,1},{6,2},{7,3},{8,12},{9,13},{10,... | collective-permute-start | bytes 786440 | tf_op jit(solution)/shard_map/ppermute | solution.py:218
  48.2 20.6 %collective-permute-done = bf16[128,1024]{1,0:T(8,128)(2,1)S(1)} collective-permute-done((bf16[128,1024]{1,0:T(8,128)(2,1)S(1)}, bf16[128,1024]{1,0:T(8,128)(2,1)S(1)}, u32[]{:S(2)}, u32[]{:S(2)}) %collective-permute-start) | collective-permute-done | bytes 262176 | tf_op jit(solution)/shard_map/ppermute | solution.py:218
  68.8 0.0 all-to-all-done
  68.9 0.7 copy-done.6
  69.6 3.1 %collective-permute-start.2 = (bf16[256,1024]{1,0:T(8,128)(2,1)S(1)}, bf16[256,1024]{1,0:T(8,128)(2,1)S(1)}, u32[]{:S(2)}, u32[]{:S(2)}) collective-permute-start(bf16[256,1024]{1,0:T(8,128)(2,1)S(1)} %constant_dynamic-update-slice_fusion.refs_8_.refs_13_), channel_id=1, source_target_pairs={{0,1},{1,2},{2,3},{3,0},{4,5},{5,6},{6,7},{7,4},{8,9},{9,10},{10,1... | collective-permute-start | bytes 1572872 | tf_op jit(solution)/shard_map/ppermute | solution.py:224
  72.7 3.6 %collective-permute-start.3 = (bf16[256,1024]{1,0:T(8,128)(2,1)S(1)}, bf16[256,1024]{1,0:T(8,128)(2,1)}, u32[]{:S(2)}, u32[]{:S(2)}) collective-permute-start(bf16[256,1024]{1,0:T(8,128)(2,1)S(1)} %constant_dynamic-update-slice_fusion.refs_8_.refs_13_), channel_id=1, source_target_pairs={{0,3},{1,0},{2,1},{3,2},{4,7},{5,4},{6,5},{7,6},{8,11},{9,8},{10,9... | collective-permute-start | bytes 1572872 | tf_op jit(solution)/shard_map/ppermute | solution.py:225
  76.3 0.7 copy.10.refs_6_.refs_7_
  77.0 5.0 %shard_map.73 = (bf16[128,1024]{1,0:T(8,128)(2,1)}, f32[128,512]{1,0:T(8,128)}) custom-call(bf16[128,1024]{1,0:T(8,128)(2,1)} %bitcast.13, bf16[1024,2048]{1,0:T(8,128)(2,1)} %bitcast.9, s32[17,128]{1,0:T(8,128)} %refs_6_.2), custom_call_target="tpu_custom_call" | custom-call | tf_op jit(solution)/shard_map/pallas_call | solution.py:168
  82.0 5.8 %shard_map.74.refs_18_ = bf16[128,1024]{1,0:T(8,128)(2,1)} custom-call(bf16[128,1024]{1,0:T(8,128)(2,1)} %bitcast.14, bf16[128,1024]{1,0:T(8,128)(2,1)} %get-tuple-element.12.refs_1_.refs_2_, bf16[128,1024]{1,0:T(8,128)(2,1)} %get-tuple-element.12.refs_1_.refs_2_, f32[128,512]{1,0:T(8,128)} %get-tuple-element.13.refs_3_, bf16[512,1024]{1,0:T(8,128)(2,1)} %bitcast.11, ...), custom_call_target="tpu_custom_call" | custom-call | tf_op jit(solution)/shard_map/pallas_call | solution.py:201
  87.8 10.9 %collective-permute-start.1 = (bf16[128,1024]{1,0:T(8,128)(2,1)}, bf16[128,1024]{1,0:T(8,128)(2,1)S(1)}, u32[]{:S(2)}, u32[]{:S(2)}) collective-permute-start(bf16[128,1024]{1,0:T(8,128)(2,1)} %shard_map.74.refs_18_), channel_id=1, source_target_pairs={{0,64},{64,128},{128,192},{192,256},{256,320},{320,384},{384,448},... | collective-permute-start | bytes 786440 | tf_op jit(solution)/shard_map/ppermute | solution.py:232
  98.7 3.4 %collective-permute-start.4 = (bf16[128,1024]{1,0:T(8,128)(2,1)S(1)}, bf16[128,1024]{1,0:T(8,128)(2,1)S(1)}, u32[]{:S(2)}, u32[]{:S(2)}) collective-permute-start(bf16[128,1024]{1,0:T(8,128)(2,1)S(1)} %bitcast.18), channel_id=1, source_target_pairs={{0,2},{1,3},{2,0},{3,1},{4,6},{5,7},{6,4},{7,5},{8,10},{9,11},{10,... | collective-permute-start | bytes 786440 | tf_op jit(solution)/shard_map/ppermute | solution.py:226
  102.2 3.4 %collective-permute-start.5 = (bf16[128,1024]{1,0:T(8,128)(2,1)S(1)}, bf16[128,1024]{1,0:T(8,128)(2,1)S(1)}, u32[]{:S(2)}, u32[]{:S(2)}) collective-permute-start(bf16[128,1024]{1,0:T(8,128)(2,1)S(1)} %copy-done.7), channel_id=1, source_target_pairs={{0,2},{1,3},{2,0},{3,1},{4,6},{5,7},{6,4},{7,5},{8,10},{9,11},{10,... | collective-permute-start | bytes 786440 | tf_op jit(solution)/shard_map/ppermute | solution.py:227
  105.6 0.7 copy-done.5
  106.3 5.1 %shard_map.75 = (bf16[128,1024]{1,0:T(8,128)(2,1)}, f32[128,512]{1,0:T(8,128)}) custom-call(bf16[128,1024]{1,0:T(8,128)(2,1)} %copy-done.5, bf16[128,1024]{1,0:T(8,128)(2,1)} %refs_1_.3, bf16[1024,2048]{1,0:T(8,128)(2,1)} %bitcast.10, s32[17,128]{1,0:T(8,128)} %refs_6_.2), custom_call_target="tpu_custom_call" | custom-call | tf_op jit(solution)/shard_map/pallas_call | solution.py:168
  111.4 0.0 collective-permute-done.4.refs_11_.refs_16_
  111.4 3.1 %collective-permute-done.5.refs_12_.refs_17_ = bf16[128,1024]{1,0:T(8,128)(2,1)S(1)} collective-permute-done((bf16[128,1024]{1,0:T(8,128)(2,1)S(1)}, bf16[128,1024]{1,0:T(8,128)(2,1)S(1)}, u32[]{:S(2)}, u32[]{:S(2)}) %collective-permute-start.5) | collective-permute-done | bytes 262176 | tf_op jit(solution)/shard_map/ppermute | solution.py:227
  114.5 0.0 collective-permute-done.2.refs_9_.refs_14_
  114.5 0.0 collective-permute-done.3.refs_10_.refs_15_
  114.5 0.7 copy-done.4
  115.2 0.2 copy-done.2
  115.4 6.3 %shard_map.76 = bf16[2,128,1024]{2,1,0:T(8,128)(2,1)} custom-call(bf16[128,1024]{1,0:T(8,128)(2,1)} %copy-done.5, bf16[128,1024]{1,0:T(8,128)(2,1)} %refs_1_.3, bf16[128,1024]{1,0:T(8,128)(2,1)} %get-tuple-element.15.refs_2_.refs_3_, bf16[128,1024]{1,0:T(8,128)(2,1)} %get-tuple-element.15.refs_2_.refs_3_, f32[128,512]{1,0:T(8,128)} %get-tuple-element.16.refs_4_, ...), custom_call_target="tpu_custom_call" | custom-call | tf_op jit(solution)/shard_map/pallas_call | solution.py:201
  (18 shorter events, 0.1 us)
Async XLA Ops:
  38.7 37.6 %copy-start.8 = (s32[17,4]{0,1:T(4,128)S(1)}, s32[17,4]{0,1:T(4,128)}, u32[]{:S(2)}) copy-start(s32[17,4]{0,1:T(4,128)} %param.13) | copy-start | bytes 820
  38.7 30.1 %all-to-all-start = ((bf16[8,128,1024]{2,1,0:T(8,128)(2,1)}), bf16[8,128,1024]{2,1,0:T(8,128)(2,1)S(1)}, u32[]{:S(2)}, u32[]{:S(2)}) async-start(bf16[8,128,1024]{2,1,0:T(8,128)(2,1)} %broadcast_in_dim.11), calls=%async_computation | async-start | bytes 4194304 | tf_op jit(solution)/shard_map/all_to_all | solution.py:220
  44.8 24.0 %collective-permute-start = (bf16[128,1024]{1,0:T(8,128)(2,1)S(1)}, bf16[128,1024]{1,0:T(8,128)(2,1)S(1)}, u32[]{:S(2)}, u32[]{:S(2)}) collective-permute-start(bf16[128,1024]{1,0:T(8,128)(2,1)S(1)} %bitcast.16), channel_id=1, source_target_pairs={{0,4},{1,5},{2,6},{3,7},{4,0},{5,1},{6,2},{7,3},{8,12},{9,13},{10,... | collective-permute-start | bytes 786440 | tf_op jit(solution)/shard_map/ppermute | solution.py:218
  68.8 0.7 copy-start.6
  68.8 13.2 %copy-start = (bf16[8,128,1024]{2,1,0:T(8,128)(2,1)}, bf16[8,128,1024]{2,1,0:T(8,128)(2,1)S(1)}, u32[]{:S(2)}) copy-start(bf16[8,128,1024]{2,1,0:T(8,128)(2,1)S(1)} %all-to-all-done) | copy-start | bytes 6291460
  69.6 12.5 %copy-start.1 = (bf16[256,1024]{1,0:T(8,128)(2,1)}, bf16[256,1024]{1,0:T(8,128)(2,1)S(1)}, u32[]{:S(2)}) copy-start(bf16[256,1024]{1,0:T(8,128)(2,1)S(1)} %constant_dynamic-update-slice_fusion.refs_8_.refs_13_) | copy-start | bytes 1572868
  69.6 44.9 %collective-permute-start.2 = (bf16[256,1024]{1,0:T(8,128)(2,1)S(1)}, bf16[256,1024]{1,0:T(8,128)(2,1)S(1)}, u32[]{:S(2)}, u32[]{:S(2)}) collective-permute-start(bf16[256,1024]{1,0:T(8,128)(2,1)S(1)} %constant_dynamic-update-slice_fusion.refs_8_.refs_13_), channel_id=1, source_target_pairs={{0,1},{1,2},{2,3},{3,0},{4,5},{5,6},{6,7},{7,4},{8,9},{9,10},{10,1... | collective-permute-start | bytes 1572872 | tf_op jit(solution)/shard_map/ppermute | solution.py:224
  72.7 41.8 %collective-permute-start.3 = (bf16[256,1024]{1,0:T(8,128)(2,1)S(1)}, bf16[256,1024]{1,0:T(8,128)(2,1)}, u32[]{:S(2)}, u32[]{:S(2)}) collective-permute-start(bf16[256,1024]{1,0:T(8,128)(2,1)S(1)} %constant_dynamic-update-slice_fusion.refs_8_.refs_13_), channel_id=1, source_target_pairs={{0,3},{1,0},{2,1},{3,2},{4,7},{5,4},{6,5},{7,6},{8,11},{9,8},{10,9... | collective-permute-start | bytes 1572872 | tf_op jit(solution)/shard_map/ppermute | solution.py:225
  82.0 20.1 %copy-start.7 = (bf16[128,1024]{1,0:T(8,128)(2,1)S(1)}, bf16[128,1024]{1,0:T(8,128)(2,1)}, u32[]{:S(2)}) copy-start(bf16[128,1024]{1,0:T(8,128)(2,1)} %copy-done.6) | copy-start | bytes 786436
  87.8 17.7 %collective-permute-start.1 = (bf16[128,1024]{1,0:T(8,128)(2,1)}, bf16[128,1024]{1,0:T(8,128)(2,1)S(1)}, u32[]{:S(2)}, u32[]{:S(2)}) collective-permute-start(bf16[128,1024]{1,0:T(8,128)(2,1)} %shard_map.74.refs_18_), channel_id=1, source_target_pairs={{0,64},{64,128},{128,192},{192,256},{256,320},{320,384},{384,448},... | collective-permute-start | bytes 786440 | tf_op jit(solution)/shard_map/ppermute | solution.py:232
  98.7 12.6 %collective-permute-start.4 = (bf16[128,1024]{1,0:T(8,128)(2,1)S(1)}, bf16[128,1024]{1,0:T(8,128)(2,1)S(1)}, u32[]{:S(2)}, u32[]{:S(2)}) collective-permute-start(bf16[128,1024]{1,0:T(8,128)(2,1)S(1)} %bitcast.18), channel_id=1, source_target_pairs={{0,2},{1,3},{2,0},{3,1},{4,6},{5,7},{6,4},{7,5},{8,10},{9,11},{10,... | collective-permute-start | bytes 786440 | tf_op jit(solution)/shard_map/ppermute | solution.py:226
  102.2 12.3 %collective-permute-start.5 = (bf16[128,1024]{1,0:T(8,128)(2,1)S(1)}, bf16[128,1024]{1,0:T(8,128)(2,1)S(1)}, u32[]{:S(2)}, u32[]{:S(2)}) collective-permute-start(bf16[128,1024]{1,0:T(8,128)(2,1)S(1)} %copy-done.7), channel_id=1, source_target_pairs={{0,2},{1,3},{2,0},{3,1},{4,6},{5,7},{6,4},{7,5},{8,10},{9,11},{10,... | collective-permute-start | bytes 786440 | tf_op jit(solution)/shard_map/ppermute | solution.py:227
  105.6 0.7 copy-start.5
  111.4 3.1 %copy-start.3 = (bf16[128,1024]{1,0:T(8,128)(2,1)}, bf16[128,1024]{1,0:T(8,128)(2,1)S(1)}, u32[]{:S(2)}) copy-start(bf16[128,1024]{1,0:T(8,128)(2,1)S(1)} %collective-permute-done.4.refs_11_.refs_16_) | copy-start | bytes 786436
  114.5 0.7 copy-start.4
  114.5 0.9 copy-start.2

commit v2 on v1

--- a/solution.py
+++ b/solution.py
@@ -6,7 +6,6 @@
 from jax.experimental import pallas as pl
 from jax.experimental.pallas import tpu as pltpu
 from jax.sharding import PartitionSpec as P
-
 
 HEADS = 4
 HD = 128
@@ -18,12 +17,9 @@
 SHARE = 16
 EVENS = [[z * NX + x for z in range(p, NZ, 2)] for p in range(2) for x in range(NX)]
 SQUARES = [[(2 * i + p) * NX + x for p in range(2) for x in range(NX)] for i in range(NZ // 2)]
-PAIR = [(c, (c // NX ^ 1) * NX + c % NX) for c in range(NX * NZ)]
+LINES = [[z * NX + x for x in range(NX)] for z in range(NZ)]
+PAIR = [(c, (c // NX + (1 if c // NX % 2 else -1)) % NZ * NX + c % NX) for c in range(NX * NZ)]
 SPAN = SHARE * NZ // 2
-
-
-def along_x(distance):
-    return [(c, (c // NX) * NX + (c % NX + distance) % NX) for c in range(NX * NZ)]
 
 
 def half_silu(half):
@@ -96,39 +92,39 @@
         uq_ref[:, :HW] = projected()
 
 
-def attend_kernel(step, n_x, sizes, *refs):
-    count = len(sizes)
-    x_refs, refs = refs[:n_x], refs[n_x:]
-    u_ref, q_ref, local_ref, w_ref, users_ref, len_ref = refs[:6]
-    key_refs, value_refs = refs[6 : 6 + count], refs[6 + count : 6 + 2 * count]
-    rest = refs[6 + 2 * count :]
-    if step > 0:
-        first_ref, out_ref, attn, masks = rest
-    else:
-        out_ref, attn, masks = rest
-    head = pl.program_id(0)
-    place = lax.axis_index("ctx")
-    x0, z0 = place % NX, place // NX
-
-    @pl.when(head == 0)
-    def _():
+def masks_kernel(users_ref, len_ref, *mask_refs):
+    n = lax.broadcasted_iota(jnp.int32, (8, SPAN), 1)
+    base = (n // SHARE) * (2 * NX * SHARE) + n % SHARE
+    for step in range(STEPS):
         batch = lax.axis_size("pipe") - 1 - lax.axis_index("pipe") + step
         bounds, total = [], 0
         for g in range(USERS - 1):
             total = total + len_ref[batch, g]
             bounds.append(total)
         _, columns = user_columns(users_ref, step)
-        n = lax.broadcasted_iota(jnp.int32, (8, SPAN), 1)
-        base = (n // SHARE) * (2 * NX * SHARE) + n % SHARE
         for b in range(2 * NX):
             if step == 0:
                 offset = b * SHARE
             else:
-                offset = ((z0 + b) % 2) * (NX * SHARE) + ((x0 + (0, 3, 1, 2)[b // 2]) % NX) * SHARE
+                offset = ((lax.axis_index("ctx") // NX + b) % 2) * (NX * SHARE) + b // 2 * SHARE
             position = base + offset
             owner = sum((position >= bound).astype(jnp.int32) for bound in bounds)
             row = jnp.broadcast_to(owner[:1].astype(jnp.float32), columns.shape)
-            masks[:, b * SPAN : (b + 1) * SPAN] = (row == columns).astype(jnp.float32)
+            mask = (row == columns).astype(jnp.float32).astype(jnp.bfloat16)
+            mask_refs[step][:, b * SPAN : (b + 1) * SPAN] = mask
+
+
+def attend_kernel(step, n_x, sizes, *refs):
+    count = len(sizes)
+    x_refs, refs = refs[:n_x], refs[n_x:]
+    u_ref, q_ref, local_ref, w_ref, masks = refs[:5]
+    key_refs, value_refs = refs[5 : 5 + count], refs[5 + count : 5 + 2 * count]
+    rest = refs[5 + 2 * count :]
+    if step > 0:
+        first_ref, out_ref, attn = rest
+    else:
+        out_ref, attn = rest
+    head = pl.program_id(0)
 
     queries = q_ref[...]
     total = local_ref[...]
@@ -137,9 +133,9 @@
         for begin in range(0, size, 2 * SPAN):
             wide = min(2 * SPAN, size - begin)
             scores = dot_t(queries, key_ref[begin : begin + wide, :])
-            weights = half_silu((0.5 * HD**-0.5) * scores) * masks[:, at : at + wide]
+            weights = half_silu((0.5 * HD**-0.5) * scores).astype(jnp.bfloat16)
             total = total + jnp.dot(
-                weights.astype(jnp.bfloat16),
+                weights * masks[:, at : at + wide],
                 value_ref[begin : begin + wide, :],
                 preferred_element_type=jnp.float32,
             )
@@ -157,6 +153,12 @@
             out_ref[1] = result
         else:
             out_ref[...] = result
+
+
+def exchange(block, groups):
+    spread = jnp.broadcast_to(block[None], (len(groups[0]), *block.shape))
+    got = lax.all_to_all(spread, "ctx", 0, 0, axis_index_groups=groups)
+    return got.reshape(-1, block.shape[-1])
 
 
 def whole(shape):
@@ -179,7 +181,18 @@
     )(*x_list, w, users)
 
 
-def attend(step, x_list, uq, local, w_back, users, lengths, rows, first=None):
+def make_masks(users, lengths):
+    shape = (users.shape[1], 2 * NX * SPAN)
+    return pl.pallas_call(
+        masks_kernel,
+        in_specs=[pl.BlockSpec(memory_space=pltpu.VMEM), pl.BlockSpec(memory_space=pltpu.SMEM)],
+        out_specs=[pl.BlockSpec(memory_space=pltpu.VMEM)] * STEPS,
+        out_shape=[jax.ShapeDtypeStruct(shape, jnp.bfloat16)] * STEPS,
+        name="masks",
+    )(users, lengths)
+
+
+def attend(step, x_list, uq, local, w_back, mask, rows, first=None):
     t, d = x_list[0].shape
     sizes = [r.shape[0] for r in rows]
     shape = (t, d) if step == 0 else (STEPS, t, d)
@@ -189,12 +202,11 @@
         pl.BlockSpec((t, HD), lambda j: (0, HEADS + j)),
         pl.BlockSpec((t, HD), lambda j: (0, j)),
         whole((HW, d)),
-        whole(users.shape),
-        pl.BlockSpec(memory_space=pltpu.SMEM),
+        whole(mask.shape),
     ]
     in_specs += [pl.BlockSpec((size, HD), lambda j: (0, j)) for size in sizes]
     in_specs += [pl.BlockSpec((size, HD), lambda j: (0, HEADS + j)) for size in sizes]
-    args = [*x_list, uq, uq, local, w_back, users, lengths, *rows, *rows]
+    args = [*x_list, uq, uq, local, w_back, mask, *rows, *rows]
     if step > 0:
         in_specs.append(whole((t, d)))
         args.append(first)
@@ -206,7 +218,6 @@
         out_shape=jax.ShapeDtypeStruct(shape, jnp.bfloat16),
         scratch_shapes=[
             pltpu.VMEM((HEADS, t, HD), jnp.float32),
-            pltpu.VMEM((t, sum(sizes)), jnp.float32),
         ],
     )(*args)
 
@@ -215,23 +226,16 @@
     w_in, w_back = w_uvqk[0], w_out[0]
     evens = lax.all_gather(cache_kv[0], "ctx", axis=0, tiled=False, axis_index_groups=EVENS)
     column = [evens[:, t].reshape(SPAN, 2 * HW) for t in range(STEPS)]
+    rows0 = exchange(column[0], SQUARES)
     other = lax.ppermute(column[1], "ctx", PAIR)
-    spread = jnp.broadcast_to(column[0][None], (2 * NX, SPAN, 2 * HW))
-    rows0 = lax.all_to_all(spread, "ctx", 0, 0, axis_index_groups=SQUARES)
-    rows0 = rows0.reshape(2 * NX * SPAN, 2 * HW)
-    mine, other, rows0 = lax.optimization_barrier((column[1], other, rows0))
-    near = jnp.concatenate([mine, other], axis=0)
-    from_left = lax.ppermute(near, "ctx", along_x(1))
-    from_right = lax.ppermute(near, "ctx", along_x(-1))
-    across = lax.ppermute(mine, "ctx", along_x(2))
-    across = [across, lax.ppermute(other, "ctx", along_x(-2))]
-    rows1 = [near, from_left, from_right, *across]
+    rows1 = exchange(jnp.concatenate([column[1], other], axis=0), LINES)
     uq, local = project(0, [incoming[0]], w_in, rows_user)
-    first = attend(0, [incoming[0]], uq, local, w_back, rows_user, cache_len, [rows0])
+    masks = make_masks(rows_user, cache_len)
+    first = attend(0, [incoming[0]], uq, local, w_back, masks[0], [rows0])
     sections = lax.axis_size("pipe")
     passed = lax.ppermute(first, "pipe", [(i, i + 1) for i in range(sections - 1)])
     uq, local = project(1, [passed, fresh], w_in, rows_user)
-    both = attend(1, [passed, fresh], uq, local, w_back, rows_user, cache_len, rows1, first)
+    both = attend(1, [passed, fresh], uq, local, w_back, masks[1], [rows1], first)
     return both[None]
 
 

time: 122 us -> 112 us (0.918)
  the two profiles are of different devices: /device:TPU:1 before, /device:TPU:34 now
where the time goes in v2:
time: 112 us; the launch traced here: 111 us
  blocking collectives  42.2 us (38%)
  Pallas kernels  23.7 us (21%)
  waiting for transfers between devices  21.3 us (19%)
  starting transfers between devices  19 us (17%)
  local copies, waits for them, and re-layouts  5.03 us (4%)
    all_gather x1, blocking collectives, body(): lax.all_gather(cache_kv[0], 'ctx', axis=0, tiled=False, axis_index_groups...  42.2 us
    all_to_all x2, starting transfers between devices, exchange(): got = lax.all_to_all(spread, 'ctx', 0, 0, axis_index_groups=groups)  12.1 us
    pallas_call x2, Pallas kernels, attend(): pl.pallas_call(functools.partial(attend_kernel, step, len(x_list), sizes)...  11.5 us
    pallas_call x2, Pallas kernels, project(): pl.pallas_call(functools.partial(project_kernel, step, len(x_list)), grid...  10.2 us
    all_to_all x2, waiting for transfers between devices, exchange(): got = lax.all_to_all(spread, 'ctx', 0, 0, axis_index_groups=groups)  9.62 us
    ppermute x1, waiting for transfers between devices, body(): lax.ppermute(first, 'pipe', [(i, i + 1) for i in range(sections - 1)])  7.18 us
    ppermute x1, starting transfers between devices, body(): other = lax.ppermute(column[1], 'ctx', PAIR)  4.94 us
    ppermute x1, waiting for transfers between devices, body(): other = lax.ppermute(column[1], 'ctx', PAIR)  4.52 us
  transfers between devices with their start and end apart: 4, of which 3 were waited for; matrix products, arithmetic and copies ran while one was open for 1% of the time, Pallas kernels for 16%

profile of v2, /device:TPU:34, one launch (start us, length us, event | category | flops | bytes accessed | tf_op | source)
XLA Modules:
  0.0 111.3 jit_solution(5711255482660619608)
XLA Ops:
  0.0 42.2 %all_gather.3 = bf16[8,2,16,1024]{3,2,1,0:T(8,128)(2,1)S(1)} all-gather(bf16[1,2,16,1024]{3,2,1,0:T(8,128)(2,1)} %param.11), channel_id=1, replica_groups={{0,8,16,24,32,40,48,56},{1,9,17,25,33,41,49,57},{2,10,18,26,34,42,50,58..., dimensions={0}, use_global_device_ids=true | all-gather | bytes 589824 | tf_op jit(solution)/shard_map/all_gather | solution.py:227
  42.3 1.6 %broadcast_in_dim.17 = bf16[8,128,1024]{2,1,0:T(8,128)(2,1)} broadcast(bf16[128,1024]{1,0:T(8,128)(2,1)S(1)} %bitcast.14), dimensions={1,2} | broadcast | bytes 2359296 | tf_op jit(solution)/shard_map/broadcast_in_dim | solution.py:159
  43.9 6.6 %all-to-all-start = ((bf16[8,128,1024]{2,1,0:T(8,128)(2,1)}), bf16[8,128,1024]{2,1,0:T(8,128)(2,1)S(1)}, u32[]{:S(2)}, u32[]{:S(2)}) async-start(bf16[8,128,1024]{2,1,0:T(8,128)(2,1)} %broadcast_in_dim.17), calls=%async_computation | async-start | bytes 4194304 | tf_op jit(solution)/shard_map/all_to_all | solution.py:160
  50.4 4.9 %collective-permute-start.1 = (bf16[128,1024]{1,0:T(8,128)(2,1)S(1)}, bf16[128,1024]{1,0:T(8,128)(2,1)S(1)}, u32[]{:S(2)}, u32[]{:S(2)}) collective-permute-start(bf16[128,1024]{1,0:T(8,128)(2,1)S(1)} %bitcast.15), channel_id=1, source_target_pairs={{0,60},{1,61},{2,62},{3,63},{4,8},{5,9},{6,10},{7,11},{8,4},{9,5},... | collective-permute-start | bytes 786440 | tf_op jit(solution)/shard_map/ppermute | solution.py:230
  55.4 4.5 %collective-permute-done.1 = bf16[128,1024]{1,0:T(8,128)(2,1)S(1)} collective-permute-done((bf16[128,1024]{1,0:T(8,128)(2,1)S(1)}, bf16[128,1024]{1,0:T(8,128)(2,1)S(1)}, u32[]{:S(2)}, u32[]{:S(2)}) %collective-permute-start.1) | collective-permute-done | bytes 262176 | tf_op jit(solution)/shard_map/ppermute | solution.py:230
  59.9 9.6 %all-to-all-done = bf16[8,128,1024]{2,1,0:T(8,128)(2,1)S(1)} async-done(((bf16[8,128,1024]{2,1,0:T(8,128)(2,1)}), bf16[8,128,1024]{2,1,0:T(8,128)(2,1)S(1)}, u32[]{:S(2)}, u32[]{:S(2)}) %all-to-all-start) | async-done | bytes 2097184 | tf_op jit(solution)/shard_map/all_to_all | solution.py:160
  69.6 0.0 copy-start
  69.6 1.8 %broadcast_in_dim.18 = bf16[4,256,1024]{2,1,0:T(8,128)(2,1)} broadcast(bf16[256,1024]{1,0:T(8,128)(2,1)S(1)} %pad_maximum_fusion), dimensions={1,2} | broadcast | bytes 2621440 | tf_op jit(solution)/shard_map/broadcast_in_dim | solution.py:159
  71.4 0.0 copy-start.2
  71.4 0.2 copy-done
  71.6 5.6 %all-to-all-start.1 = ((bf16[4,256,1024]{2,1,0:T(8,128)(2,1)}), bf16[4,256,1024]{2,1,0:T(8,128)(2,1)}, u32[]{:S(2)}, u32[]{:S(2)}) async-start(bf16[4,256,1024]{2,1,0:T(8,128)(2,1)} %broadcast_in_dim.18), calls=%async_computation.1 | async-start | bytes 4194304 | tf_op jit(solution)/shard_map/all_to_all | solution.py:160
  77.1 0.0 copy-done.2
  77.1 0.7 copy.9.len_ref
  77.8 2.0 %masks.1 = (bf16[128,1024]{1,0:T(8,128)(2,1)}, bf16[128,1024]{1,0:T(8,128)(2,1)}) custom-call(s32[17,128]{1,0:T(8,128)} %refs_3_.1, s32[17,4]{1,0:T(8,128)} %copy.9.len_ref), custom_call_target="tpu_custom_call" | custom-call | tf_op jit(solution)/shard_map/masks/pallas_call | solution.py:186
  79.8 5.0 %shard_map.73 = (bf16[128,1024]{1,0:T(8,128)(2,1)}, f32[128,512]{1,0:T(8,128)}) custom-call(bf16[128,1024]{1,0:T(8,128)(2,1)} %bitcast.17, bf16[1024,2048]{1,0:T(8,128)(2,1)} %bitcast.10, s32[17,128]{1,0:T(8,128)} %refs_3_.1), custom_call_target="tpu_custom_call" | custom-call | tf_op jit(solution)/shard_map/pallas_call | solution.py:170
  84.8 5.6 %shard_map.74.refs_9_ = bf16[128,1024]{1,0:T(8,128)(2,1)} custom-call(bf16[128,1024]{1,0:T(8,128)(2,1)} %bitcast.18, bf16[128,1024]{1,0:T(8,128)(2,1)} %get-tuple-element.11.refs_1_.refs_2_, bf16[128,1024]{1,0:T(8,128)(2,1)} %get-tuple-element.11.refs_1_.refs_2_, f32[128,512]{1,0:T(8,128)} %get-tuple-element.12.refs_3_, bf16[512,1024]{1,0:T(8,128)(2,1)} %bitcast.12, ...), custom_call_target="tpu_custom_call" | custom-call | tf_op jit(solution)/shard_map/pallas_call | solution.py:213
  90.5 1.9 %collective-permute-start = (bf16[128,1024]{1,0:T(8,128)(2,1)}, bf16[128,1024]{1,0:T(8,128)(2,1)S(1)}, u32[]{:S(2)}, u32[]{:S(2)}) collective-permute-start(bf16[128,1024]{1,0:T(8,128)(2,1)} %shard_map.74.refs_9_), channel_id=1, source_target_pairs={{0,64},{64,128},{128,192},{192,256},{256,320},{320,384},{384,448},... | collective-permute-start | bytes 786440 | tf_op jit(solution)/shard_map/ppermute | solution.py:236
  92.4 7.2 %collective-permute-done.refs_0_ = bf16[128,1024]{1,0:T(8,128)(2,1)S(1)} collective-permute-done((bf16[128,1024]{1,0:T(8,128)(2,1)}, bf16[128,1024]{1,0:T(8,128)(2,1)S(1)}, u32[]{:S(2)}, u32[]{:S(2)}) %collective-permute-start) | collective-permute-done | bytes 262176 | tf_op jit(solution)/shard_map/ppermute | solution.py:236
  99.6 0.0 copy-start.1
  99.6 0.7 copy-done.1
  100.3 5.1 %shard_map.75 = (bf16[128,1024]{1,0:T(8,128)(2,1)}, f32[128,512]{1,0:T(8,128)}) custom-call(bf16[128,1024]{1,0:T(8,128)(2,1)} %copy-done.1, bf16[128,1024]{1,0:T(8,128)(2,1)} %refs_1_.3, bf16[1024,2048]{1,0:T(8,128)(2,1)} %bitcast.11, s32[17,128]{1,0:T(8,128)} %refs_3_.1), custom_call_target="tpu_custom_call" | custom-call | tf_op jit(solution)/shard_map/pallas_call | solution.py:170
  105.4 0.0 all-to-all-done.1
  105.4 5.9 %shard_map.76 = bf16[2,128,1024]{2,1,0:T(8,128)(2,1)} custom-call(bf16[128,1024]{1,0:T(8,128)(2,1)} %copy-done.1, bf16[128,1024]{1,0:T(8,128)(2,1)} %refs_1_.3, bf16[128,1024]{1,0:T(8,128)(2,1)} %get-tuple-element.14.refs_2_.refs_3_, bf16[128,1024]{1,0:T(8,128)(2,1)} %get-tuple-element.14.refs_2_.refs_3_, f32[128,512]{1,0:T(8,128)} %get-tuple-element.15.refs_4_, ...), custom_call_target="tpu_custom_call" | custom-call | tf_op jit(solution)/shard_map/pallas_call | solution.py:213
  (2 shorter events, 0.1 us)
Async XLA Ops:
  43.9 25.7 %all-to-all-start = ((bf16[8,128,1024]{2,1,0:T(8,128)(2,1)}), bf16[8,128,1024]{2,1,0:T(8,128)(2,1)S(1)}, u32[]{:S(2)}, u32[]{:S(2)}) async-start(bf16[8,128,1024]{2,1,0:T(8,128)(2,1)} %broadcast_in_dim.17), calls=%async_computation | async-start | bytes 4194304 | tf_op jit(solution)/shard_map/all_to_all | solution.py:160
  50.4 9.5 %collective-permute-start.1 = (bf16[128,1024]{1,0:T(8,128)(2,1)S(1)}, bf16[128,1024]{1,0:T(8,128)(2,1)S(1)}, u32[]{:S(2)}, u32[]{:S(2)}) collective-permute-start(bf16[128,1024]{1,0:T(8,128)(2,1)S(1)} %bitcast.15), channel_id=1, source_target_pairs={{0,60},{1,61},{2,62},{3,63},{4,8},{5,9},{6,10},{7,11},{8,4},{9,5},... | collective-permute-start | bytes 786440 | tf_op jit(solution)/shard_map/ppermute | solution.py:230
  69.6 2.0 %copy-start = (bf16[8,128,1024]{2,1,0:T(8,128)(2,1)}, bf16[8,128,1024]{2,1,0:T(8,128)(2,1)S(1)}, u32[]{:S(2)}) copy-start(bf16[8,128,1024]{2,1,0:T(8,128)(2,1)S(1)} %all-to-all-done) | copy-start | bytes 6291460
  71.4 5.8 %copy-start.2 = (s32[17,4]{0,1:T(4,128)S(1)}, s32[17,4]{0,1:T(4,128)}, u32[]{:S(2)}) copy-start(s32[17,4]{0,1:T(4,128)} %param.13) | copy-start | bytes 820
  71.6 33.9 %all-to-all-start.1 = ((bf16[4,256,1024]{2,1,0:T(8,128)(2,1)}), bf16[4,256,1024]{2,1,0:T(8,128)(2,1)}, u32[]{:S(2)}, u32[]{:S(2)}) async-start(bf16[4,256,1024]{2,1,0:T(8,128)(2,1)} %broadcast_in_dim.18), calls=%async_computation.1 | async-start | bytes 4194304 | tf_op jit(solution)/shard_map/all_to_all | solution.py:160
  90.5 9.1 %collective-permute-start = (bf16[128,1024]{1,0:T(8,128)(2,1)}, bf16[128,1024]{1,0:T(8,128)(2,1)S(1)}, u32[]{:S(2)}, u32[]{:S(2)}) collective-permute-start(bf16[128,1024]{1,0:T(8,128)(2,1)} %shard_map.74.refs_9_), channel_id=1, source_target_pairs={{0,64},{64,128},{128,192},{192,256},{256,320},{320,384},{384,448},... | collective-permute-start | bytes 786440 | tf_op jit(solution)/shard_map/ppermute | solution.py:236
  99.6 0.7 copy-start.1

commit v3 on v0

v3 whole, which is shorter than its diff:
```python
import functools

import jax
import jax.numpy as jnp
from jax import lax
from jax.experimental import pallas as pl
from jax.experimental.pallas import tpu as pltpu
from jax.sharding import PartitionSpec as P


HEADS = 4
HD = 128
HW = HEADS * HD
STEPS = 2
NX = 4
NZ = 16
USERS = 4
SHARE = 16
EVENS = [[z * NX + x for z in range(p, NZ, 2)] for p in range(2) for x in range(NX)]
SQUARES = [[(2 * i + p) * NX + x for p in range(2) for x in range(NX)] for i in range(NZ // 2)]
PAIR = [(c, (c // NX + (1 if c // NX % 2 else -1)) % NZ * NX + c % NX) for c in range(NX * NZ)]
HOPS = (0, 3, 1, 2)
SPAN = SHARE * NZ // 2


def along_x(distance):
    return [(c, (c // NX) * NX + (c % NX + distance) % NX) for c in range(NX * NZ)]


def half_silu(half):
    return half + half * jnp.tanh(half)


def normalize(values):
    center = jnp.mean(values, axis=-1, keepdims=True)
    shifted = values - center
    spread = jnp.mean(shifted * shifted, axis=-1, keepdims=True)
    return shifted * lax.rsqrt(spread + 1e-06)


def dot_t(a, b):
    return lax.dot_general(a, b, (((1,), (1,)), ((), ())), preferred_element_type=jnp.float32)


def user_columns(users_ref, step):
    batch = lax.axis_size("pipe") - 1 - lax.axis_index("pipe") + step
    row = users_ref[pl.ds(batch, 1), :].astype(jnp.float32)
    square = jnp.broadcast_to(row, (row.shape[1], row.shape[1]))
    return square, square.T


def current_of(refs, step):
    if step == 0:
        return refs[0][...]
    passed, fresh = refs
    return jnp.where(lax.axis_index("pipe") == 0, fresh[...], passed[...])


def project_kernel(step, *refs):
    passed, (w_hbm, x_ref, users_ref, uq_ref, attn_ref, w_ref, arrived) = refs[:step], refs[step:]
    x_refs = (*passed, x_ref)
    fetches = [
        pltpu.make_async_copy(
            w_hbm.at[:, pl.ds(part * HW, HW)], w_ref.at[part], arrived.at[part]
        )
        for part in range(4)
    ]
    for part in (1, 2, 3, 0):
        fetches[part].start()
    normed = normalize(current_of(x_refs, step).astype(jnp.float32)).astype(jnp.bfloat16)

    def projected(part):
        fetches[part].wait()
        wide = jnp.dot(normed, w_ref[part], preferred_element_type=jnp.float32)
        return half_silu(0.5 * wide).astype(jnp.bfloat16)

    queries, keys, values = projected(1), projected(2), projected(3)
    uq_ref[:, HW:] = queries
    rows, columns = user_columns(users_ref, step)
    t = lax.broadcasted_iota(jnp.int32, rows.shape, 0)
    n = lax.broadcasted_iota(jnp.int32, rows.shape, 1)
    allowed = (rows == columns) & (n <= t)
    for h in range(HEADS):
        s = slice(h * HD, (h + 1) * HD)
        scores = dot_t(queries[:, s], keys[:, s])
        weights = jnp.where(allowed, half_silu((0.5 * HD**-0.5) * scores), 0.0)
        attn_ref[:, s] = jnp.dot(
            weights.astype(jnp.bfloat16), values[:, s], preferred_element_type=jnp.float32
        )
    uq_ref[:, :HW] = projected(0)


def masks_kernel(step, users_ref, len_ref, mask_ref):
    batch = lax.axis_size("pipe") - 1 - lax.axis_index("pipe") + step
    lengths = len_ref[pl.ds(batch, 1), :]
    n = lax.broadcasted_iota(jnp.int32, (8, SPAN), 1)
    base = (n // SHARE) * (2 * NX * SHARE) + n % SHARE
    bounds = [lengths[:, 0:1]]
    for g in range(1, USERS - 1):
        bounds.append(bounds[-1] + lengths[:, g : g + 1])
    bounds = [jnp.broadcast_to(bound, base.shape) for bound in bounds]
    _, columns = user_columns(users_ref, step)
    for b in range(2 * NX):
        if step == 0:
            offset = b * SHARE
        else:
            x, z = lax.axis_index("ctx") % NX, lax.axis_index("ctx") // NX
            offset = (z + b) % 2 * (NX * SHARE) + (x + HOPS[b // 2]) % NX * SHARE
        position = base + offset
        owner = sum((position >= bound).astype(jnp.int32) for bound in bounds)
        row = jnp.broadcast_to(owner[:1].astype(jnp.float32), columns.shape)
        mask = (row == columns).astype(jnp.float32).astype(jnp.bfloat16)
        mask_ref[:, b * SPAN : (b + 1) * SPAN] = mask


def attend_kernel(step, sizes, *refs):
    row_refs, w_ref, refs = refs[: len(sizes)], refs[len(sizes)], refs[len(sizes) + 1 :]
    if step > 0:
        passed, uq_ref, local_ref, x_ref, mask_ref, *rest = refs
        x_refs = (passed, x_ref)
    else:
        x_ref, uq_ref, local_ref, mask_ref, *rest = refs
        x_refs = (x_ref,)
    attn = []
    for h in range(HEADS):
        key_part, value_part = slice(h * HD, (h + 1) * HD), slice(HW + h * HD, HW + (h + 1) * HD)
        queries = uq_ref[:, value_part]
        total = local_ref[:, key_part]
        at = 0
        for row_ref, size in zip(row_refs, sizes):
            for begin in range(0, size, 2 * SPAN):
                wide = min(2 * SPAN, size - begin)
                scores = dot_t(queries, row_ref[begin : begin + wide, key_part])
                weights = half_silu((0.5 * HD**-0.5) * scores).astype(jnp.bfloat16)
                total = total + jnp.dot(
                    weights * mask_ref[:, at : at + wide],
                    row_ref[begin : begin + wide, value_part],
                    preferred_element_type=jnp.float32,
                )
                at += wide
        attn.append(total)
    whole = jnp.concatenate(attn, axis=1)
    mixed = (normalize(whole) * uq_ref[:, :HW].astype(jnp.float32)).astype(jnp.bfloat16)
    result = jnp.dot(mixed, w_ref[...], preferred_element_type=jnp.float32)
    result = (result + current_of(x_refs, step).astype(jnp.float32)).astype(jnp.bfloat16)
    if step > 0:
        first_ref, out_ref = rest
        out_ref[0] = first_ref[...]
        out_ref[1] = result
    else:
        rest[0][...] = result


def exchange(block, groups):
    spread = jnp.broadcast_to(block[None], (len(groups[0]), *block.shape))
    got = lax.all_to_all(spread, "ctx", 0, 0, axis_index_groups=groups)
    return got.reshape(-1, block.shape[-1])


RESIDENT = pl.BlockSpec(memory_space=pltpu.VMEM)


def fetched_spec(value):
    return pl.BlockSpec(value.shape, lambda j: (0,) * len(value.shape))


def call(kernel, outs, kept, fetched, lean=16, stay=(), scratch=()):
    keep = not any(isinstance(out, jax.ShapeDtypeStruct) for out in outs)
    return pl.pallas_call(
        kernel,
        grid=(1,),
        in_specs=[RESIDENT for _ in kept]
        + [pl.BlockSpec(memory_space=pltpu.HBM) for _ in stay]
        + [fetched_spec(value) for value in fetched],
        out_specs=[RESIDENT if keep else fetched_spec(out) for out in outs],
        out_shape=outs,
        scratch_shapes=list(scratch),
        compiler_params=pltpu.CompilerParams(vmem_limit_bytes=lean << 20 if lean else None),
    )(*[pltpu.with_memory_space_constraint(value, pltpu.VMEM) for value in kept], *stay, *fetched)


def project(step, x_list, w, users):
    t = x_list[0].shape[0]
    kind = pltpu.VMEM if step > 0 else jax.ShapeDtypeStruct
    outs = [kind((t, 2 * HW), jnp.bfloat16), kind((t, HW), jnp.float32)]
    kernel = functools.partial(project_kernel, step)
    scratch = [pltpu.VMEM((4, w.shape[0], HW), w.dtype), pltpu.SemaphoreType.DMA((4,))]
    kept, fetched = x_list[:step], [x_list[step], users]
    return call(kernel, outs, kept, fetched, lean=60 * step, stay=[w], scratch=scratch)


def make_mask(step, users, lengths):
    outs = [jax.ShapeDtypeStruct((users.shape[1], 2 * NX * SPAN), jnp.bfloat16)]
    kernel = functools.partial(masks_kernel, step)
    return call(kernel, outs, [], [users, lengths], lean=16 * step)[0]


def attend(step, x_list, uq, local, w_back, mask, rows, first=()):
    t, d = x_list[0].shape
    sizes = [r.shape[0] for r in rows]
    kernel = functools.partial(attend_kernel, step, sizes)
    if step > 0:
        outs = [jax.ShapeDtypeStruct((STEPS, t, d), jnp.bfloat16)]
        kept = [*rows, w_back, x_list[0], uq, local]
        return call(kernel, outs, kept, [x_list[1], mask, *first])[0]
    outs = [pltpu.VMEM((t, d), jnp.bfloat16)]
    fetched = [*x_list, uq, local, mask]
    return call(kernel, outs, [*rows, w_back], fetched, lean=0)[0]


def body(incoming, fresh, w_uvqk, w_out, cache_kv, rows_user, cache_len):
    w_in, w_back = w_uvqk[0], w_out[0]
    evens = lax.all_gather(cache_kv[0], "ctx", axis=0, tiled=False, axis_index_groups=EVENS)
    column = [evens[:, t].reshape(SPAN, 2 * HW) for t in range(STEPS)]
    rows0 = exchange(column[0], SQUARES)
    other = lax.ppermute(column[1], "ctx", PAIR)
    near = jnp.concatenate([column[1], other], axis=0)
    rows1 = [near, lax.ppermute(near, "ctx", along_x(1))]
    rows1.append(lax.ppermute(near, "ctx", along_x(-1)))
    rows1.append(lax.ppermute(column[1], "ctx", along_x(2)))
    rows1.append(lax.ppermute(other, "ctx", along_x(-2)))
    uq, local = project(0, [incoming[0]], w_in, rows_user)
    mask0 = make_mask(0, rows_user, cache_len)
    mask1 = make_mask(1, rows_user, cache_len)
    first = attend(0, [incoming[0]], uq, local, w_back, mask0, [rows0])
    sections = lax.axis_size("pipe")
    passed = lax.ppermute(first, "pipe", [(i, i + 1) for i in range(sections - 1)])
    uq, local = project(1, [passed, fresh], w_in, rows_user)
    both = attend(1, [passed, fresh], uq, local, w_back, mask1, rows1, [first])
    return both[None]


def solution(mesh):
    in_specs = (
        P("pipe", "ctx", None),
        P("ctx", None),
        P("pipe", None, None),
        P("pipe", None, None),
        P("pipe", None, "ctx", None),
        P(None, "ctx"),
        P(),
    )
    out_specs = P("pipe", None, "ctx", None)
    return jax.shard_map(body, mesh=mesh, in_specs=in_specs, out_specs=out_specs, check_vma=False)
```

time: 349 us -> 103 us (0.30)
  the two profiles are of different devices: /device:TPU:8 before, /device:TPU:1 now
where the time goes in v3:
time: 103 us
  blocking collectives  37.1 us (36%)
  starting transfers between devices  33.7 us (33%)
  Pallas kernels  17.9 us (17%)
  waiting for transfers between devices  10.6 us (10%)
  local copies, waits for them, and re-layouts  2.37 us (2%)
    all_gather x1, blocking collectives, body(): lax.all_gather(cache_kv[0], 'ctx', axis=0, tiled=False, axis_index_groups...  37.1 us
    pallas_call x6, Pallas kernels, call(): pl.pallas_call(kernel, grid=(1,), in_specs=[RESIDENT for _ in kept] + [pl...  17.9 us
    ppermute x1, starting transfers between devices, body(): lax.ppermute(first, 'pipe', [(i, i + 1) for i in range(sections - 1)])  9.53 us
    all_to_all x1, starting transfers between devices, exchange(): got = lax.all_to_all(spread, 'ctx', 0, 0, axis_index_groups=groups)  6.1 us
    ppermute x1, starting transfers between devices, body(): other = lax.ppermute(column[1], 'ctx', PAIR)  4.85 us
    ppermute x1, waiting for transfers between devices, body(): rows1.append(lax.ppermute(other, 'ctx', along_x(-2)))  4.01 us
    ppermute x1, waiting for transfers between devices, body(): other = lax.ppermute(column[1], 'ctx', PAIR)  3.75 us
    ppermute x1, starting transfers between devices, body(): rows1.append(lax.ppermute(column[1], 'ctx', along_x(2)))  3.57 us
  transfers between devices with their start and end apart: 7, of which 4 were waited for; matrix products, arithmetic and copies ran while one was open for 2% of the time, Pallas kernels for 13%

profile of v3, /device:TPU:1, one launch (start us, length us, event | category | flops | bytes accessed | tf_op | source)
XLA Modules:
  0.0 102.7 jit_solution(13439482222932557753)
XLA Ops:
  0.0 37.1 %all_gather.3 = bf16[8,2,16,1024]{3,2,1,0:T(8,128)(2,1)S(1)} all-gather(bf16[1,2,16,1024]{3,2,1,0:T(8,128)(2,1)} %param.11), channel_id=1, replica_groups={{0,8,16,24,32,40,48,56},{1,9,17,25,33,41,49,57},{2,10,18,26,34,42,50,58..., dimensions={0}, use_global_device_ids=true | all-gather | bytes 589824 | tf_op jit(solution)/shard_map/all_gather | solution.py:213
  37.1 0.0 copy-start.4
  37.1 1.6 %broadcast_in_dim.11 = bf16[8,128,1024]{2,1,0:T(8,128)(2,1)} broadcast(bf16[128,1024]{1,0:T(8,128)(2,1)S(1)} %bitcast.14), dimensions={1,2} | broadcast | bytes 2359296 | tf_op jit(solution)/shard_map/broadcast_in_dim | solution.py:155
  38.8 6.1 %all-to-all-start = ((bf16[8,128,1024]{2,1,0:T(8,128)(2,1)}), bf16[8,128,1024]{2,1,0:T(8,128)(2,1)S(1)}, u32[]{:S(2)}, u32[]{:S(2)}) async-start(bf16[8,128,1024]{2,1,0:T(8,128)(2,1)} %broadcast_in_dim.11), calls=%async_computation | async-start | bytes 4194304 | tf_op jit(solution)/shard_map/all_to_all | solution.py:156
  44.8 4.9 %collective-permute-start = (bf16[128,1024]{1,0:T(8,128)(2,1)S(1)}, bf16[128,1024]{1,0:T(8,128)(2,1)S(1)}, u32[]{:S(2)}, u32[]{:S(2)}) collective-permute-start(bf16[128,1024]{1,0:T(8,128)(2,1)S(1)} %bitcast.15), channel_id=1, source_target_pairs={{0,60},{1,61},{2,62},{3,63},{4,8},{5,9},{6,10},{7,11},{8,4},{9,5},... | collective-permute-start | bytes 786440 | tf_op jit(solution)/shard_map/ppermute | solution.py:216
  49.7 3.7 %collective-permute-done = bf16[128,1024]{1,0:T(8,128)(2,1)S(1)} collective-permute-done((bf16[128,1024]{1,0:T(8,128)(2,1)S(1)}, bf16[128,1024]{1,0:T(8,128)(2,1)S(1)}, u32[]{:S(2)}, u32[]{:S(2)}) %collective-permute-start) | collective-permute-done | bytes 262176 | tf_op jit(solution)/shard_map/ppermute | solution.py:216
  53.5 0.9 pad_maximum_fusion.refs_0_
  54.4 3.1 %collective-permute-start.1 = (bf16[256,1024]{1,0:T(8,128)(2,1)}, bf16[256,1024]{1,0:T(8,128)(2,1)}, u32[]{:S(2)}, u32[]{:S(2)}) collective-permute-start(bf16[256,1024]{1,0:T(8,128)(2,1)} %pad_maximum_fusion.refs_0_), channel_id=1, source_target_pairs={{0,1},{1,2},{2,3},{3,0},{4,5},{5,6},{6,7},{7,4},{8,9},{9,10},{10,1... | collective-permute-start | bytes 1572872 | tf_op jit(solution)/shard_map/ppermute | solution.py:218
  57.5 3.4 %collective-permute-start.2 = (bf16[256,1024]{1,0:T(8,128)(2,1)}, bf16[256,1024]{1,0:T(8,128)(2,1)}, u32[]{:S(2)}, u32[]{:S(2)}) collective-permute-start(bf16[256,1024]{1,0:T(8,128)(2,1)} %pad_maximum_fusion.refs_0_), channel_id=1, source_target_pairs={{0,3},{1,0},{2,1},{3,2},{4,7},{5,4},{6,5},{7,6},{8,11},{9,8},{10,9... | collective-permute-start | bytes 1572872 | tf_op jit(solution)/shard_map/ppermute | solution.py:219
  60.9 0.7 copy.10.len_ref
  61.6 1.6 %shard_map.74.refs_5_ = bf16[128,1024]{1,0:T(8,128)(2,1)} custom-call(s32[17,128]{1,0:T(8,128)} %users_ref.3, s32[17,4]{1,0:T(8,128)} %copy.10.len_ref), custom_call_target="tpu_custom_call" | custom-call | tf_op jit(solution)/shard_map/pallas_call | solution.py:169
  63.2 4.8 %shard_map.73 = (bf16[128,1024]{1,0:T(8,128)(2,1)}, f32[128,512]{1,0:T(8,128)}) custom-call(bf16[1024,2048]{1,0:T(8,128)(2,1)} %bitcast.10, bf16[128,1024]{1,0:T(8,128)(2,1)} %bitcast.12, s32[17,128]{1,0:T(8,128)} %users_ref.3), custom_call_target="tpu_custom_call" | custom-call | tf_op jit(solution)/shard_map/pallas_call | solution.py:169
  68.0 2.1 %all-to-all-done = bf16[8,128,1024]{2,1,0:T(8,128)(2,1)S(1)} async-done(((bf16[8,128,1024]{2,1,0:T(8,128)(2,1)}), bf16[8,128,1024]{2,1,0:T(8,128)(2,1)S(1)}, u32[]{:S(2)}, u32[]{:S(2)}) %all-to-all-start) | async-done | bytes 2097184 | tf_op jit(solution)/shard_map/all_to_all | solution.py:156
  70.1 2.7 %shard_map.75.refs_11_ = bf16[128,1024]{1,0:T(8,128)(2,1)S(1)} custom-call(bf16[1024,1024]{1,0:T(8,128)(2,1)S(1)} %bitcast.7, bf16[512,1024]{1,0:T(8,128)(2,1)S(1)} %bitcast.8, bf16[128,1024]{1,0:T(8,128)(2,1)} %bitcast.13, bf16[128,1024]{1,0:T(8,128)(2,1)} %get-tuple-element.9.refs_3_, f32[128,512]{1,0:T(8,128)} %get-tuple-element.10.refs_4_, ...), custom_call_target="tpu_custom_call" | custom-call | tf_op jit(solution)/shard_map/pallas_call | solution.py:169
  72.8 9.5 %collective-permute-start.5 = (bf16[128,1024]{1,0:T(8,128)(2,1)S(1)}, bf16[128,1024]{1,0:T(8,128)(2,1)S(1)}, u32[]{:S(2)}, u32[]{:S(2)}) collective-permute-start(bf16[128,1024]{1,0:T(8,128)(2,1)S(1)} %shard_map.75.refs_11_), channel_id=1, source_target_pairs={{0,64},{64,128},{128,192},{192,256},{256,320},{320,384},{384,448},... | collective-permute-start | bytes 786440 | tf_op jit(solution)/shard_map/ppermute | solution.py:227
  82.3 3.6 %collective-permute-start.3 = (bf16[128,1024]{1,0:T(8,128)(2,1)}, bf16[128,1024]{1,0:T(8,128)(2,1)S(1)}, u32[]{:S(2)}, u32[]{:S(2)}) collective-permute-start(bf16[128,1024]{1,0:T(8,128)(2,1)} %bitcast.17), channel_id=1, source_target_pairs={{0,2},{1,3},{2,0},{3,1},{4,6},{5,7},{6,4},{7,5},{8,10},{9,11},{10,... | collective-permute-start | bytes 786440 | tf_op jit(solution)/shard_map/ppermute | solution.py:220
  85.9 3.2 %collective-permute-start.4 = (bf16[128,1024]{1,0:T(8,128)(2,1)}, bf16[128,1024]{1,0:T(8,128)(2,1)S(1)}, u32[]{:S(2)}, u32[]{:S(2)}) collective-permute-start(bf16[128,1024]{1,0:T(8,128)(2,1)} %copy-done.5), channel_id=1, source_target_pairs={{0,2},{1,3},{2,0},{3,1},{4,6},{5,7},{6,4},{7,5},{8,10},{9,11},{10,... | collective-permute-start | bytes 786440 | tf_op jit(solution)/shard_map/ppermute | solution.py:221
  89.1 0.2 shard_map.77.refs_10_
  89.3 0.0 copy-start.1
  89.3 0.0 collective-permute-done.5.refs_0_.refs_6_
  89.3 4.1 %shard_map.76 = (bf16[128,1024]{1,0:T(8,128)(2,1)S(1)}, f32[128,512]{1,0:T(8,128)S(1)}) custom-call(bf16[128,1024]{1,0:T(8,128)(2,1)S(1)} %collective-permute-done.5.refs_0_.refs_6_, bf16[1024,2048]{1,0:T(8,128)(2,1)} %bitcast.11, bf16[128,1024]{1,0:T(8,128)(2,1)} %refs_9_.1, s32[17,128]{1,0:T(8,128)} %users_ref.3), custom_call_target="tpu_custom_call" | custom-call | tf_op jit(solution)/shard_map/pallas_call | solution.py:169
  93.5 0.8 collective-permute-done.3.refs_3_
  94.2 4.0 %collective-permute-done.4.refs_4_ = bf16[128,1024]{1,0:T(8,128)(2,1)S(1)} collective-permute-done((bf16[128,1024]{1,0:T(8,128)(2,1)}, bf16[128,1024]{1,0:T(8,128)(2,1)S(1)}, u32[]{:S(2)}, u32[]{:S(2)}) %collective-permute-start.4) | collective-permute-done | bytes 262176 | tf_op jit(solution)/shard_map/ppermute | solution.py:221
  98.3 4.5 %shard_map.78 = bf16[2,128,1024]{2,1,0:T(8,128)(2,1)} custom-call(bf16[256,1024]{1,0:T(8,128)(2,1)} %pad_maximum_fusion.refs_0_, bf16[256,1024]{1,0:T(8,128)(2,1)} %collective-permute-done.1.refs_1_, bf16[256,1024]{1,0:T(8,128)(2,1)} %collective-permute-done.2.refs_2_, bf16[128,1024]{1,0:T(8,128)(2,1)S(1)} %collective-permute-done.3.refs_3_, ...), custom_call_target="tpu_custom_call" | custom-call | tf_op jit(solution)/shard_map/pallas_call | solution.py:169
  (15 shorter events, 0.1 us)
Async XLA Ops:
  37.1 16.3 %copy-start.4 = (bf16[8,1,16,1024]{3,2,1,0:T(8,128)(2,1)}, bf16[8,1,16,1024]{3,2,1,0:T(8,128)(2,1)S(1)}, u32[]{:S(2)}) copy-start(bf16[8,1,16,1024]{3,2,1,0:T(8,128)(2,1)S(1)} %get-tuple-element.14) | copy-start | bytes 786436
  38.7 22.1 %copy-start.6 = (s32[17,4]{0,1:T(4,128)S(1)}, s32[17,4]{0,1:T(4,128)}, u32[]{:S(2)}) copy-start(s32[17,4]{0,1:T(4,128)} %param.13) | copy-start | bytes 820
  38.8 31.3 %all-to-all-start = ((bf16[8,128,1024]{2,1,0:T(8,128)(2,1)}), bf16[8,128,1024]{2,1,0:T(8,128)(2,1)S(1)}, u32[]{:S(2)}, u32[]{:S(2)}) async-start(bf16[8,128,1024]{2,1,0:T(8,128)(2,1)} %broadcast_in_dim.11), calls=%async_computation | async-start | bytes 4194304 | tf_op jit(solution)/shard_map/all_to_all | solution.py:156
  44.8 8.6 %collective-permute-start = (bf16[128,1024]{1,0:T(8,128)(2,1)S(1)}, bf16[128,1024]{1,0:T(8,128)(2,1)S(1)}, u32[]{:S(2)}, u32[]{:S(2)}) collective-permute-start(bf16[128,1024]{1,0:T(8,128)(2,1)S(1)} %bitcast.15), channel_id=1, source_target_pairs={{0,60},{1,61},{2,62},{3,63},{4,8},{5,9},{6,10},{7,11},{8,4},{9,5},... | collective-permute-start | bytes 786440 | tf_op jit(solution)/shard_map/ppermute | solution.py:216
  53.5 9.7 %copy-start.5 = (bf16[128,1024]{1,0:T(8,128)(2,1)}, bf16[128,1024]{1,0:T(8,128)(2,1)S(1)}, u32[]{:S(2)}) copy-start(bf16[128,1024]{1,0:T(8,128)(2,1)S(1)} %collective-permute-done) | copy-start | bytes 786436
  54.4 43.9 %collective-permute-start.1 = (bf16[256,1024]{1,0:T(8,128)(2,1)}, bf16[256,1024]{1,0:T(8,128)(2,1)}, u32[]{:S(2)}, u32[]{:S(2)}) collective-permute-start(bf16[256,1024]{1,0:T(8,128)(2,1)} %pad_maximum_fusion.refs_0_), channel_id=1, source_target_pairs={{0,1},{1,2},{2,3},{3,0},{4,5},{5,6},{6,7},{7,4},{8,9},{9,10},{10,1... | collective-permute-start | bytes 1572872 | tf_op jit(solution)/shard_map/ppermute | solution.py:218
  57.5 40.8 %collective-permute-start.2 = (bf16[256,1024]{1,0:T(8,128)(2,1)}, bf16[256,1024]{1,0:T(8,128)(2,1)}, u32[]{:S(2)}, u32[]{:S(2)}) collective-permute-start(bf16[256,1024]{1,0:T(8,128)(2,1)} %pad_maximum_fusion.refs_0_), channel_id=1, source_target_pairs={{0,3},{1,0},{2,1},{3,2},{4,7},{5,4},{6,5},{7,6},{8,11},{9,8},{10,9... | collective-permute-start | bytes 1572872 | tf_op jit(solution)/shard_map/ppermute | solution.py:219
  63.2 6.9 %copy-start = (bf16[1,512,1024]{2,1,0:T(8,128)(2,1)S(1)}, bf16[1,512,1024]{2,1,0:T(8,128)(2,1)}, u32[]{:S(2)}) copy-start(bf16[1,512,1024]{2,1,0:T(8,128)(2,1)} %param.10) | copy-start | bytes 3145732
  70.1 19.0 %copy-start.2 = (s32[17,128]{1,0:T(8,128)S(1)}, s32[17,128]{1,0:T(8,128)}, u32[]{:S(2)}) copy-start(s32[17,128]{1,0:T(8,128)} %users_ref.3) | copy-start | bytes 26116
  70.1 19.0 %copy-start.3 = (s32[17,4]{1,0:T(8,128)S(1)}, s32[17,4]{1,0:T(8,128)}, u32[]{:S(2)}) copy-start(s32[17,4]{1,0:T(8,128)} %copy.10.len_ref) | copy-start | bytes 820
  72.8 16.6 %collective-permute-start.5 = (bf16[128,1024]{1,0:T(8,128)(2,1)S(1)}, bf16[128,1024]{1,0:T(8,128)(2,1)S(1)}, u32[]{:S(2)}, u32[]{:S(2)}) collective-permute-start(bf16[128,1024]{1,0:T(8,128)(2,1)S(1)} %shard_map.75.refs_11_), channel_id=1, source_target_pairs={{0,64},{64,128},{128,192},{192,256},{256,320},{320,384},{384,448},... | collective-permute-start | bytes 786440 | tf_op jit(solution)/shard_map/ppermute | solution.py:227
  82.3 11.9 %collective-permute-start.3 = (bf16[128,1024]{1,0:T(8,128)(2,1)}, bf16[128,1024]{1,0:T(8,128)(2,1)S(1)}, u32[]{:S(2)}, u32[]{:S(2)}) collective-permute-start(bf16[128,1024]{1,0:T(8,128)(2,1)} %bitcast.17), channel_id=1, source_target_pairs={{0,2},{1,3},{2,0},{3,1},{4,6},{5,7},{6,4},{7,5},{8,10},{9,11},{10,... | collective-permute-start | bytes 786440 | tf_op jit(solution)/shard_map/ppermute | solution.py:220
  85.9 12.4 %collective-permute-start.4 = (bf16[128,1024]{1,0:T(8,128)(2,1)}, bf16[128,1024]{1,0:T(8,128)(2,1)S(1)}, u32[]{:S(2)}, u32[]{:S(2)}) collective-permute-start(bf16[128,1024]{1,0:T(8,128)(2,1)} %copy-done.5), channel_id=1, source_target_pairs={{0,2},{1,3},{2,0},{3,1},{4,6},{5,7},{6,4},{7,5},{8,10},{9,11},{10,... | collective-permute-start | bytes 786440 | tf_op jit(solution)/shard_map/ppermute | solution.py:221
  89.3 8.9 %copy-start.1 = (bf16[128,1024]{1,0:T(8,128)(2,1)S(1)}, bf16[128,1024]{1,0:T(8,128)(2,1)}, u32[]{:S(2)}) copy-start(bf16[128,1024]{1,0:T(8,128)(2,1)} %refs_9_.1) | copy-start | bytes 786436

commit v4 on v3

--- a/solution.py
+++ b/solution.py
@@ -92,12 +92,13 @@
 
 def masks_kernel(step, users_ref, len_ref, mask_ref):
     batch = lax.axis_size("pipe") - 1 - lax.axis_index("pipe") + step
-    lengths = len_ref[pl.ds(batch, 1), :]
+    column = lax.broadcasted_iota(jnp.int32, len_ref.shape, 1) == batch
+    lengths = jnp.sum(jnp.where(column, len_ref[...], 0), axis=1, keepdims=True)
     n = lax.broadcasted_iota(jnp.int32, (8, SPAN), 1)
     base = (n // SHARE) * (2 * NX * SHARE) + n % SHARE
-    bounds = [lengths[:, 0:1]]
+    bounds = [lengths[0:1]]
     for g in range(1, USERS - 1):
-        bounds.append(bounds[-1] + lengths[:, g : g + 1])
+        bounds.append(bounds[-1] + lengths[g : g + 1])
     bounds = [jnp.broadcast_to(bound, base.shape) for bound in bounds]
     _, columns = user_columns(users_ref, step)
     for b in range(2 * NX):
@@ -113,33 +114,43 @@
         mask_ref[:, b * SPAN : (b + 1) * SPAN] = mask
 
 
-def attend_kernel(step, sizes, *refs):
-    row_refs, w_ref, refs = refs[: len(sizes)], refs[len(sizes)], refs[len(sizes) + 1 :]
+def gathered(at, uq_ref, local_ref, mask_ref, row_refs):
+    attn = []
+    for h in range(HEADS):
+        key_part, value_part = slice(h * HD, (h + 1) * HD), slice(HW + h * HD, HW + (h + 1) * HD)
+        queries = uq_ref[:, value_part]
+        total = local_ref[:, key_part]
+        begin_at = at
+        for row_ref in row_refs:
+            size = row_ref.shape[0]
+            for begin in range(0, size, 2 * SPAN):
+                wide = min(2 * SPAN, size - begin)
+                scores = dot_t(queries, row_ref[begin : begin + wide, key_part])
+                weights = half_silu((0.5 * HD**-0.5) * scores).astype(jnp.bfloat16)
+                total = total + jnp.dot(
+                    weights * mask_ref[:, begin_at : begin_at + wide],
+                    row_ref[begin : begin + wide, value_part],
+                    preferred_element_type=jnp.float32,
+                )
+                begin_at += wide
+        attn.append(total)
+    return jnp.concatenate(attn, axis=1)
+
+
+def early_kernel(*refs):
+    *row_refs, uq_ref, local_ref, mask_ref, out_ref = refs
+    out_ref[...] = gathered(0, uq_ref, local_ref, mask_ref, row_refs)
+
+
+def attend_kernel(step, at, count, *refs):
+    row_refs, w_ref, refs = refs[:count], refs[count], refs[count + 1 :]
     if step > 0:
         passed, uq_ref, local_ref, x_ref, mask_ref, *rest = refs
         x_refs = (passed, x_ref)
     else:
         x_ref, uq_ref, local_ref, mask_ref, *rest = refs
         x_refs = (x_ref,)
-    attn = []
-    for h in range(HEADS):
-        key_part, value_part = slice(h * HD, (h + 1) * HD), slice(HW + h * HD, HW + (h + 1) * HD)
-        queries = uq_ref[:, value_part]
-        total = local_ref[:, key_part]
-        at = 0
-        for row_ref, size in zip(row_refs, sizes):
-            for begin in range(0, size, 2 * SPAN):
-                wide = min(2 * SPAN, size - begin)
-                scores = dot_t(queries, row_ref[begin : begin + wide, key_part])
-                weights = half_silu((0.5 * HD**-0.5) * scores).astype(jnp.bfloat16)
-                total = total + jnp.dot(
-                    weights * mask_ref[:, at : at + wide],
-                    row_ref[begin : begin + wide, value_part],
-                    preferred_element_type=jnp.float32,
-                )
-                at += wide
-        attn.append(total)
-    whole = jnp.concatenate(attn, axis=1)
+    whole = gathered(at, uq_ref, local_ref, mask_ref, row_refs)
     mixed = (normalize(whole) * uq_ref[:, :HW].astype(jnp.float32)).astype(jnp.bfloat16)
     result = jnp.dot(mixed, w_ref[...], preferred_element_type=jnp.float32)
     result = (result + current_of(x_refs, step).astype(jnp.float32)).astype(jnp.bfloat16)
@@ -195,10 +206,14 @@
     return call(kernel, outs, [], [users, lengths], lean=16 * step)[0]
 
 
-def attend(step, x_list, uq, local, w_back, mask, rows, first=()):
+def attend_early(uq, local, mask, rows):
+    outs = [pltpu.VMEM(local.shape, jnp.float32)]
+    return call(early_kernel, outs, [*rows, uq, local], [mask])[0]
+
+
+def attend(step, x_list, uq, local, w_back, mask, rows, at=0, first=()):
     t, d = x_list[0].shape
-    sizes = [r.shape[0] for r in rows]
-    kernel = functools.partial(attend_kernel, step, sizes)
+    kernel = functools.partial(attend_kernel, step, at, len(rows))
     if step > 0:
         outs = [jax.ShapeDtypeStruct((STEPS, t, d), jnp.bfloat16)]
         kept = [*rows, w_back, x_list[0], uq, local]
@@ -220,13 +235,15 @@
     rows1.append(lax.ppermute(column[1], "ctx", along_x(2)))
     rows1.append(lax.ppermute(other, "ctx", along_x(-2)))
     uq, local = project(0, [incoming[0]], w_in, rows_user)
-    mask0 = make_mask(0, rows_user, cache_len)
-    mask1 = make_mask(1, rows_user, cache_len)
+    mask0 = make_mask(0, rows_user, cache_len.T)
+    mask1 = make_mask(1, rows_user, cache_len.T)
     first = attend(0, [incoming[0]], uq, local, w_back, mask0, [rows0])
     sections = lax.axis_size("pipe")
     passed = lax.ppermute(first, "pipe", [(i, i + 1) for i in range(sections - 1)])
     uq, local = project(1, [passed, fresh], w_in, rows_user)
-    both = attend(1, [passed, fresh], uq, local, w_back, mask1, rows1, [first])
+    local = attend_early(uq, local, mask1, rows1[:-1])
+    at = 2 * NX * SPAN - rows1[-1].shape[0]
+    both = attend(1, [passed, fresh], uq, local, w_back, mask1, rows1[-1:], at, [first])
     return both[None]
 
 

time: 103 us -> 99.9 us (0.970)
  waiting for transfers between devices: 10.6 us -> 8.63 us
    ppermute x1, waiting for transfers between devices: 4.01 us -> 1.29 us  [body(): rows1.append(lax.ppermute(other, 'ctx', along_x(-2)))]
    pallas_call x6 -> x7, Pallas kernels: 17.9 us -> 18.1 us  [call(): pl.pallas_call(kernel, grid=(1,), in_specs=[RESIDENT for _ in kept] + [pl...]
  transfers between devices with their start and end apart: 7 -> 7, of which waited for: 4 -> 4; matrix products, arithmetic and copies ran while one was open for 2% -> 1% of each run, Pallas kernels for 13% -> 16%
where the time goes in v4:
time: 99.9 us; the launch traced here: 99.4 us
  blocking collectives  37.1 us (37%)
  starting transfers between devices  32.9 us (33%)
  Pallas kernels  18.1 us (18%)
  waiting for transfers between devices  8.63 us (9%)
  local copies, waits for them, and re-layouts  1.65 us (2%)
    all_gather x1, blocking collectives, body(): lax.all_gather(cache_kv[0], 'ctx', axis=0, tiled=False, axis_index_groups...  37.1 us
    pallas_call x7, Pallas kernels, call(): pl.pallas_call(kernel, grid=(1,), in_specs=[RESIDENT for _ in kept] + [pl...  18.1 us
    ppermute x1, starting transfers between devices, body(): lax.ppermute(first, 'pipe', [(i, i + 1) for i in range(sections - 1)])  8.81 us
    all_to_all x1, starting transfers between devices, exchange(): got = lax.all_to_all(spread, 'ctx', 0, 0, axis_index_groups=groups)  5.97 us
    ppermute x1, starting transfers between devices, body(): other = lax.ppermute(column[1], 'ctx', PAIR)  4.85 us
    ppermute x1, waiting for transfers between devices, body(): other = lax.ppermute(column[1], 'ctx', PAIR)  3.75 us
    ppermute x1, starting transfers between devices, body(): rows1.append(lax.ppermute(column[1], 'ctx', along_x(2)))  3.56 us
    ppermute x1, starting transfers between devices, body(): rows1.append(lax.ppermute(near, 'ctx', along_x(-1)))  3.4 us
  transfers between devices with their start and end apart: 7, of which 4 were waited for; matrix products, arithmetic and copies ran while one was open for 1% of the time, Pallas kernels for 16%

profile of v4, /device:TPU:1, one launch (start us, length us, event | category | flops | bytes accessed | tf_op | source)
XLA Modules:
  0.0 99.4 jit_solution(13113912726559695979)
XLA Ops:
  0.0 37.1 %all_gather.3 = bf16[8,2,16,1024]{3,2,1,0:T(8,128)(2,1)S(1)} all-gather(bf16[1,2,16,1024]{3,2,1,0:T(8,128)(2,1)} %param.11), channel_id=1, replica_groups={{0,8,16,24,32,40,48,56},{1,9,17,25,33,41,49,57},{2,10,18,26,34,42,50,58..., dimensions={0}, use_global_device_ids=true | all-gather | bytes 589824 | tf_op jit(solution)/shard_map/all_gather | solution.py:228
  37.1 1.6 %broadcast_in_dim.11 = bf16[8,128,1024]{2,1,0:T(8,128)(2,1)} broadcast(bf16[128,1024]{1,0:T(8,128)(2,1)S(1)} %bitcast.17), dimensions={1,2} | broadcast | bytes 2359296 | tf_op jit(solution)/shard_map/broadcast_in_dim | solution.py:166
  38.7 6.0 %all-to-all-start = ((bf16[8,128,1024]{2,1,0:T(8,128)(2,1)}), bf16[8,128,1024]{2,1,0:T(8,128)(2,1)S(1)}, u32[]{:S(2)}, u32[]{:S(2)}) async-start(bf16[8,128,1024]{2,1,0:T(8,128)(2,1)} %broadcast_in_dim.11), calls=%async_computation | async-start | bytes 4194304 | tf_op jit(solution)/shard_map/all_to_all | solution.py:167
  44.7 4.9 %collective-permute-start = (bf16[128,1024]{1,0:T(8,128)(2,1)S(1)}, bf16[128,1024]{1,0:T(8,128)(2,1)S(1)}, u32[]{:S(2)}, u32[]{:S(2)}) collective-permute-start(bf16[128,1024]{1,0:T(8,128)(2,1)S(1)} %bitcast.18), channel_id=1, source_target_pairs={{0,60},{1,61},{2,62},{3,63},{4,8},{5,9},{6,10},{7,11},{8,4},{9,5},... | collective-permute-start | bytes 786440 | tf_op jit(solution)/shard_map/ppermute | solution.py:231
  49.6 3.7 %collective-permute-done = bf16[128,1024]{1,0:T(8,128)(2,1)S(1)} collective-permute-done((bf16[128,1024]{1,0:T(8,128)(2,1)S(1)}, bf16[128,1024]{1,0:T(8,128)(2,1)S(1)}, u32[]{:S(2)}, u32[]{:S(2)}) %collective-permute-start) | collective-permute-done | bytes 262176 | tf_op jit(solution)/shard_map/ppermute | solution.py:231
  53.3 0.9 pad_maximum_fusion.refs_0_
  54.2 3.1 %collective-permute-start.3 = (bf16[256,1024]{1,0:T(8,128)(2,1)}, bf16[256,1024]{1,0:T(8,128)(2,1)}, u32[]{:S(2)}, u32[]{:S(2)}) collective-permute-start(bf16[256,1024]{1,0:T(8,128)(2,1)} %pad_maximum_fusion.refs_0_), channel_id=1, source_target_pairs={{0,1},{1,2},{2,3},{3,0},{4,5},{5,6},{6,7},{7,4},{8,9},{9,10},{10,1... | collective-permute-start | bytes 1572872 | tf_op jit(solution)/shard_map/ppermute | solution.py:233
  57.3 3.4 %collective-permute-start.4 = (bf16[256,1024]{1,0:T(8,128)(2,1)}, bf16[256,1024]{1,0:T(8,128)(2,1)}, u32[]{:S(2)}, u32[]{:S(2)}) collective-permute-start(bf16[256,1024]{1,0:T(8,128)(2,1)} %pad_maximum_fusion.refs_0_), channel_id=1, source_target_pairs={{0,3},{1,0},{2,1},{3,2},{4,7},{5,4},{6,5},{7,6},{8,11},{9,8},{10,9... | collective-permute-start | bytes 1572872 | tf_op jit(solution)/shard_map/ppermute | solution.py:234
  60.7 1.6 %shard_map.74.refs_5_ = bf16[128,1024]{1,0:T(8,128)(2,1)} custom-call(s32[17,128]{1,0:T(8,128)} %users_ref.3, s32[4,17]{1,0:T(4,128)} %bitcast.11), custom_call_target="tpu_custom_call" | custom-call | tf_op jit(solution)/shard_map/pallas_call | solution.py:180
  62.3 4.8 %shard_map.73 = (bf16[128,1024]{1,0:T(8,128)(2,1)}, f32[128,512]{1,0:T(8,128)}) custom-call(bf16[1024,2048]{1,0:T(8,128)(2,1)} %bitcast.13, bf16[128,1024]{1,0:T(8,128)(2,1)} %bitcast.15, s32[17,128]{1,0:T(8,128)} %users_ref.3), custom_call_target="tpu_custom_call" | custom-call | tf_op jit(solution)/shard_map/pallas_call | solution.py:180
  67.2 2.8 %all-to-all-done = bf16[8,128,1024]{2,1,0:T(8,128)(2,1)S(1)} async-done(((bf16[8,128,1024]{2,1,0:T(8,128)(2,1)}), bf16[8,128,1024]{2,1,0:T(8,128)(2,1)S(1)}, u32[]{:S(2)}, u32[]{:S(2)}) %all-to-all-start) | async-done | bytes 2097184 | tf_op jit(solution)/shard_map/all_to_all | solution.py:167
  70.0 2.7 %shard_map.75.refs_7_ = bf16[128,1024]{1,0:T(8,128)(2,1)S(1)} custom-call(bf16[1024,1024]{1,0:T(8,128)(2,1)S(1)} %bitcast.8, bf16[512,1024]{1,0:T(8,128)(2,1)S(1)} %bitcast.9, bf16[128,1024]{1,0:T(8,128)(2,1)} %bitcast.16, bf16[128,1024]{1,0:T(8,128)(2,1)} %get-tuple-element.9.refs_3_, f32[128,512]{1,0:T(8,128)} %get-tuple-element.10.refs_4_, ...), custom_call_target="tpu_custom_call" | custom-call | tf_op jit(solution)/shard_map/pallas_call | solution.py:180
  72.6 8.8 %collective-permute-start.2 = (bf16[128,1024]{1,0:T(8,128)(2,1)S(1)}, bf16[128,1024]{1,0:T(8,128)(2,1)S(1)}, u32[]{:S(2)}, u32[]{:S(2)}) collective-permute-start(bf16[128,1024]{1,0:T(8,128)(2,1)S(1)} %shard_map.75.refs_7_), channel_id=1, source_target_pairs={{0,64},{64,128},{128,192},{192,256},{256,320},{320,384},{384,448},... | collective-permute-start | bytes 786440 | tf_op jit(solution)/shard_map/ppermute | solution.py:242
  81.5 3.6 %collective-permute-start.5 = (bf16[128,1024]{1,0:T(8,128)(2,1)}, bf16[128,1024]{1,0:T(8,128)(2,1)S(1)}, u32[]{:S(2)}, u32[]{:S(2)}) collective-permute-start(bf16[128,1024]{1,0:T(8,128)(2,1)} %bitcast.20), channel_id=1, source_target_pairs={{0,2},{1,3},{2,0},{3,1},{4,6},{5,7},{6,4},{7,5},{8,10},{9,11},{10,... | collective-permute-start | bytes 786440 | tf_op jit(solution)/shard_map/ppermute | solution.py:235
  85.0 3.2 %collective-permute-start.1 = (bf16[128,1024]{1,0:T(8,128)(2,1)}, bf16[128,1024]{1,0:T(8,128)(2,1)S(1)}, u32[]{:S(2)}, u32[]{:S(2)}) collective-permute-start(bf16[128,1024]{1,0:T(8,128)(2,1)} %copy-done.5), channel_id=1, source_target_pairs={{0,2},{1,3},{2,0},{3,1},{4,6},{5,7},{6,4},{7,5},{8,10},{9,11},{10,... | collective-permute-start | bytes 786440 | tf_op jit(solution)/shard_map/ppermute | solution.py:236
  88.3 0.2 shard_map.77.refs_6_
  88.5 0.0 collective-permute-done.2.refs_0_.refs_2_
  88.5 4.1 %shard_map.76 = (bf16[128,1024]{1,0:T(8,128)(2,1)S(1)}, f32[128,512]{1,0:T(8,128)S(1)}) custom-call(bf16[128,1024]{1,0:T(8,128)(2,1)S(1)} %collective-permute-done.2.refs_0_.refs_2_, bf16[1024,2048]{1,0:T(8,128)(2,1)} %bitcast.14, bf16[128,1024]{1,0:T(8,128)(2,1)} %refs_5_.1, s32[17,128]{1,0:T(8,128)} %users_ref.3), custom_call_target="tpu_custom_call" | custom-call | tf_op jit(solution)/shard_map/pallas_call | solution.py:180
  92.6 0.0 copy-start.1
  92.6 0.8 collective-permute-done.5.refs_3_
  93.4 0.0 collective-permute-done.3.refs_1_
  93.4 2.7 %shard_map.78.refs_4_ = f32[128,512]{1,0:T(8,128)S(1)} custom-call(bf16[256,1024]{1,0:T(8,128)(2,1)} %pad_maximum_fusion.refs_0_, bf16[256,1024]{1,0:T(8,128)(2,1)} %collective-permute-done.3.refs_1_, bf16[256,1024]{1,0:T(8,128)(2,1)} %collective-permute-done.4.refs_2_, bf16[128,1024]{1,0:T(8,128)(2,1)S(1)} %collective-permute-done.5.refs_3_, ...), custom_call_target="tpu_custom_call" | custom-call | tf_op jit(solution)/shard_map/pallas_call | solution.py:180
  96.1 1.3 %collective-permute-done.1.refs_0_ = bf16[128,1024]{1,0:T(8,128)(2,1)S(1)} collective-permute-done((bf16[128,1024]{1,0:T(8,128)(2,1)}, bf16[128,1024]{1,0:T(8,128)(2,1)S(1)}, u32[]{:S(2)}, u32[]{:S(2)}) %collective-permute-start.1) | collective-permute-done | bytes 262176 | tf_op jit(solution)/shard_map/ppermute | solution.py:236
  97.4 2.0 %shard_map.79 = bf16[2,128,1024]{2,1,0:T(8,128)(2,1)} custom-call(bf16[128,1024]{1,0:T(8,128)(2,1)S(1)} %collective-permute-done.1.refs_0_, bf16[512,1024]{1,0:T(8,128)(2,1)S(1)} %bitcast.10, bf16[128,1024]{1,0:T(8,128)(2,1)S(1)} %collective-permute-done.2.refs_0_.refs_2_, bf16[128,1024]{1,0:T(8,128)(2,1)S(1)} %get-tuple-element.11.refs_4_.refs_3_, ...), custom_call_target="tpu_custom_call" | custom-call | tf_op jit(solution)/shard_map/pallas_call | solution.py:180
  (13 shorter events, 0.1 us)
Async XLA Ops:
  37.1 16.2 %copy-start.4 = (bf16[8,1,16,1024]{3,2,1,0:T(8,128)(2,1)}, bf16[8,1,16,1024]{3,2,1,0:T(8,128)(2,1)S(1)}, u32[]{:S(2)}) copy-start(bf16[8,1,16,1024]{3,2,1,0:T(8,128)(2,1)S(1)} %get-tuple-element.14) | copy-start | bytes 786436
  38.7 31.2 %all-to-all-start = ((bf16[8,128,1024]{2,1,0:T(8,128)(2,1)}), bf16[8,128,1024]{2,1,0:T(8,128)(2,1)S(1)}, u32[]{:S(2)}, u32[]{:S(2)}) async-start(bf16[8,128,1024]{2,1,0:T(8,128)(2,1)} %broadcast_in_dim.11), calls=%async_computation | async-start | bytes 4194304 | tf_op jit(solution)/shard_map/all_to_all | solution.py:167
  44.7 8.6 %collective-permute-start = (bf16[128,1024]{1,0:T(8,128)(2,1)S(1)}, bf16[128,1024]{1,0:T(8,128)(2,1)S(1)}, u32[]{:S(2)}, u32[]{:S(2)}) collective-permute-start(bf16[128,1024]{1,0:T(8,128)(2,1)S(1)} %bitcast.18), channel_id=1, source_target_pairs={{0,60},{1,61},{2,62},{3,63},{4,8},{5,9},{6,10},{7,11},{8,4},{9,5},... | collective-permute-start | bytes 786440 | tf_op jit(solution)/shard_map/ppermute | solution.py:231
  53.3 9.0 %copy-start.5 = (bf16[128,1024]{1,0:T(8,128)(2,1)}, bf16[128,1024]{1,0:T(8,128)(2,1)S(1)}, u32[]{:S(2)}) copy-start(bf16[128,1024]{1,0:T(8,128)(2,1)S(1)} %collective-permute-done) | copy-start | bytes 786436
  54.2 39.2 %collective-permute-start.3 = (bf16[256,1024]{1,0:T(8,128)(2,1)}, bf16[256,1024]{1,0:T(8,128)(2,1)}, u32[]{:S(2)}, u32[]{:S(2)}) collective-permute-start(bf16[256,1024]{1,0:T(8,128)(2,1)} %pad_maximum_fusion.refs_0_), channel_id=1, source_target_pairs={{0,1},{1,2},{2,3},{3,0},{4,5},{5,6},{6,7},{7,4},{8,9},{9,10},{10,1... | collective-permute-start | bytes 1572872 | tf_op jit(solution)/shard_map/ppermute | solution.py:233
  57.3 36.1 %collective-permute-start.4 = (bf16[256,1024]{1,0:T(8,128)(2,1)}, bf16[256,1024]{1,0:T(8,128)(2,1)}, u32[]{:S(2)}, u32[]{:S(2)}) collective-permute-start(bf16[256,1024]{1,0:T(8,128)(2,1)} %pad_maximum_fusion.refs_0_), channel_id=1, source_target_pairs={{0,3},{1,0},{2,1},{3,2},{4,7},{5,4},{6,5},{7,6},{8,11},{9,8},{10,9... | collective-permute-start | bytes 1572872 | tf_op jit(solution)/shard_map/ppermute | solution.py:234
  62.3 7.6 %copy-start = (bf16[1,512,1024]{2,1,0:T(8,128)(2,1)S(1)}, bf16[1,512,1024]{2,1,0:T(8,128)(2,1)}, u32[]{:S(2)}) copy-start(bf16[1,512,1024]{2,1,0:T(8,128)(2,1)} %param.10) | copy-start | bytes 3145732
  70.0 18.3 %copy-start.2 = (s32[17,128]{1,0:T(8,128)S(1)}, s32[17,128]{1,0:T(8,128)}, u32[]{:S(2)}) copy-start(s32[17,128]{1,0:T(8,128)} %users_ref.3) | copy-start | bytes 26116
  70.0 18.3 %copy-start.3 = (s32[17,4]{0,1:T(4,128)S(1)}, s32[17,4]{0,1:T(4,128)}, u32[]{:S(2)}) copy-start(s32[17,4]{0,1:T(4,128)} %param.13) | copy-start | bytes 820
  72.6 15.9 %collective-permute-start.2 = (bf16[128,1024]{1,0:T(8,128)(2,1)S(1)}, bf16[128,1024]{1,0:T(8,128)(2,1)S(1)}, u32[]{:S(2)}, u32[]{:S(2)}) collective-permute-start(bf16[128,1024]{1,0:T(8,128)(2,1)S(1)} %shard_map.75.refs_7_), channel_id=1, source_target_pairs={{0,64},{64,128},{128,192},{192,256},{256,320},{320,384},{384,448},... | collective-permute-start | bytes 786440 | tf_op jit(solution)/shard_map/ppermute | solution.py:242
  81.5 11.9 %collective-permute-start.5 = (bf16[128,1024]{1,0:T(8,128)(2,1)}, bf16[128,1024]{1,0:T(8,128)(2,1)S(1)}, u32[]{:S(2)}, u32[]{:S(2)}) collective-permute-start(bf16[128,1024]{1,0:T(8,128)(2,1)} %bitcast.20), channel_id=1, source_target_pairs={{0,2},{1,3},{2,0},{3,1},{4,6},{5,7},{6,4},{7,5},{8,10},{9,11},{10,... | collective-permute-start | bytes 786440 | tf_op jit(solution)/shard_map/ppermute | solution.py:235
  85.0 12.4 %collective-permute-start.1 = (bf16[128,1024]{1,0:T(8,128)(2,1)}, bf16[128,1024]{1,0:T(8,128)(2,1)S(1)}, u32[]{:S(2)}, u32[]{:S(2)}) collective-permute-start(bf16[128,1024]{1,0:T(8,128)(2,1)} %copy-done.5), channel_id=1, source_target_pairs={{0,2},{1,3},{2,0},{3,1},{4,6},{5,7},{6,4},{7,5},{8,10},{9,11},{10,... | collective-permute-start | bytes 786440 | tf_op jit(solution)/shard_map/ppermute | solution.py:236
  92.6 4.8 %copy-start.1 = (bf16[128,1024]{1,0:T(8,128)(2,1)S(1)}, bf16[128,1024]{1,0:T(8,128)(2,1)}, u32[]{:S(2)}) copy-start(bf16[128,1024]{1,0:T(8,128)(2,1)} %refs_5_.1) | copy-start | bytes 786436

commit v5 on v4

--- a/solution.py
+++ b/solution.py
@@ -90,7 +90,7 @@
     uq_ref[:, :HW] = projected(0)
 
 
-def masks_kernel(step, users_ref, len_ref, mask_ref):
+def fill_mask(step, users_ref, len_ref, mask_ref):
     batch = lax.axis_size("pipe") - 1 - lax.axis_index("pipe") + step
     column = lax.broadcasted_iota(jnp.int32, len_ref.shape, 1) == batch
     lengths = jnp.sum(jnp.where(column, len_ref[...], 0), axis=1, keepdims=True)
@@ -148,8 +148,9 @@
         passed, uq_ref, local_ref, x_ref, mask_ref, *rest = refs
         x_refs = (passed, x_ref)
     else:
-        x_ref, uq_ref, local_ref, mask_ref, *rest = refs
+        x_ref, uq_ref, local_ref, users_ref, len_ref, *rest, mask_ref = refs
         x_refs = (x_ref,)
+        fill_mask(step, users_ref, len_ref, mask_ref)
     whole = gathered(at, uq_ref, local_ref, mask_ref, row_refs)
     mixed = (normalize(whole) * uq_ref[:, :HW].astype(jnp.float32)).astype(jnp.bfloat16)
     result = jnp.dot(mixed, w_ref[...], preferred_element_type=jnp.float32)
@@ -202,7 +203,7 @@
 
 def make_mask(step, users, lengths):
     outs = [jax.ShapeDtypeStruct((users.shape[1], 2 * NX * SPAN), jnp.bfloat16)]
-    kernel = functools.partial(masks_kernel, step)
+    kernel = functools.partial(fill_mask, step)
     return call(kernel, outs, [], [users, lengths], lean=16 * step)[0]
 
 
@@ -219,8 +220,10 @@
         kept = [*rows, w_back, x_list[0], uq, local]
         return call(kernel, outs, kept, [x_list[1], mask, *first])[0]
     outs = [pltpu.VMEM((t, d), jnp.bfloat16)]
-    fetched = [*x_list, uq, local, mask]
-    return call(kernel, outs, [*rows, w_back], fetched, lean=0)[0]
+    fetched = [*x_list, uq, local, *mask]
+    scratch = [pltpu.VMEM((t, rows[0].shape[0]), jnp.bfloat16)]
+    kept = [*rows, w_back]
+    return call(kernel, outs, kept, fetched, lean=0, scratch=scratch)[0]
 
 
 def body(incoming, fresh, w_uvqk, w_out, cache_kv, rows_user, cache_len):
@@ -230,14 +233,14 @@
     rows0 = exchange(column[0], SQUARES)
     other = lax.ppermute(column[1], "ctx", PAIR)
     near = jnp.concatenate([column[1], other], axis=0)
+    mine = lax.optimization_barrier(evens)[:, 1].reshape(SPAN, 2 * HW)
     rows1 = [near, lax.ppermute(near, "ctx", along_x(1))]
     rows1.append(lax.ppermute(near, "ctx", along_x(-1)))
-    rows1.append(lax.ppermute(column[1], "ctx", along_x(2)))
+    rows1.append(lax.ppermute(mine, "ctx", along_x(2)))
     rows1.append(lax.ppermute(other, "ctx", along_x(-2)))
     uq, local = project(0, [incoming[0]], w_in, rows_user)
-    mask0 = make_mask(0, rows_user, cache_len.T)
     mask1 = make_mask(1, rows_user, cache_len.T)
-    first = attend(0, [incoming[0]], uq, local, w_back, mask0, [rows0])
+    first = attend(0, [incoming[0]], uq, local, w_back, (rows_user, cache_len.T), [rows0])
     sections = lax.axis_size("pipe")
     passed = lax.ppermute(first, "pipe", [(i, i + 1) for i in range(sections - 1)])
     uq, local = project(1, [passed, fresh], w_in, rows_user)

time: 99.9 us -> 99.8 us (level)
  local copies, waits for them, and re-layouts: 1.65 us -> 3.45 us
  Pallas kernels: 18.1 us -> 16.4 us
  starting transfers between devices: 32.9 us -> 31.3 us
  waiting for transfers between devices: 8.63 us -> 10 us
    pallas_call x7 -> x6, Pallas kernels: 18.1 us -> 16.4 us  [call(): pl.pallas_call(kernel, grid=(1,), in_specs=[RESIDENT for _ in kept] + [pl...]
    all_to_all x1, waiting for transfers between devices: 2.79 us -> 4.41 us  [exchange(): got = lax.all_to_all(spread, 'ctx', 0, 0, axis_index_groups=groups)]
    ppermute x1, starting transfers between devices: 8.81 us -> 7.2 us  [body(): lax.ppermute(first, 'pipe', [(i, i + 1) for i in range(sections - 1)])]
  transfers between devices with their start and end apart: 7 -> 7, of which waited for: 4 -> 4; matrix products, arithmetic and copies ran while one was open for 1% -> 2% of each run, Pallas kernels for 16% -> 15%
where the time goes in v5:
time: 99.8 us; the launch traced here: 99.3 us
  blocking collectives  37.1 us (37%)
  starting transfers between devices  31.3 us (31%)
  Pallas kernels  16.4 us (16%)
  waiting for transfers between devices  10 us (10%)
  local copies, waits for them, and re-layouts  3.45 us (3%)
    all_gather x1, blocking collectives, body(): lax.all_gather(cache_kv[0], 'ctx', axis=0, tiled=False, axis_index_groups...  37.1 us
    pallas_call x6, Pallas kernels, call(): pl.pallas_call(kernel, grid=(1,), in_specs=[RESIDENT for _ in kept] + [pl...  16.4 us
    ppermute x1, starting transfers between devices, body(): lax.ppermute(first, 'pipe', [(i, i + 1) for i in range(sections - 1)])  7.2 us
    all_to_all x1, starting transfers between devices, exchange(): got = lax.all_to_all(spread, 'ctx', 0, 0, axis_index_groups=groups)  5.97 us
    ppermute x1, starting transfers between devices, body(): other = lax.ppermute(column[1], 'ctx', PAIR)  4.85 us
    all_to_all x1, waiting for transfers between devices, exchange(): got = lax.all_to_all(spread, 'ctx', 0, 0, axis_index_groups=groups)  4.41 us
    ppermute x1, waiting for transfers between devices, body(): other = lax.ppermute(column[1], 'ctx', PAIR)  3.75 us
    ppermute x1, starting transfers between devices, body(): rows1.append(lax.ppermute(mine, 'ctx', along_x(2)))  3.56 us
  transfers between devices with their start and end apart: 7, of which 4 were waited for; matrix products, arithmetic and copies ran while one was open for 2% of the time, Pallas kernels for 15%

profile of v5, /device:TPU:1, one launch (start us, length us, event | category | flops | bytes accessed | tf_op | source)
XLA Modules:
  0.0 99.3 jit_solution(8625966382744175697)
XLA Ops:
  0.0 37.1 %all_gather.3 = bf16[8,2,16,1024]{3,2,1,0:T(8,128)(2,1)S(1)} all-gather(bf16[1,2,16,1024]{3,2,1,0:T(8,128)(2,1)} %param.11), channel_id=1, replica_groups={{0,8,16,24,32,40,48,56},{1,9,17,25,33,41,49,57},{2,10,18,26,34,42,50,58..., dimensions={0}, use_global_device_ids=true | all-gather | bytes 589824 | tf_op jit(solution)/shard_map/all_gather | solution.py:231
  37.1 0.8 copy-done.4
  37.9 1.6 %broadcast_in_dim.11 = bf16[8,128,1024]{2,1,0:T(8,128)(2,1)} broadcast(bf16[128,1024]{1,0:T(8,128)(2,1)S(1)} %bitcast.18), dimensions={1,2} | broadcast | bytes 2359296 | tf_op jit(solution)/shard_map/broadcast_in_dim | solution.py:167
  39.5 6.0 %all-to-all-start = ((bf16[8,128,1024]{2,1,0:T(8,128)(2,1)}), bf16[8,128,1024]{2,1,0:T(8,128)(2,1)S(1)}, u32[]{:S(2)}, u32[]{:S(2)}) async-start(bf16[8,128,1024]{2,1,0:T(8,128)(2,1)} %broadcast_in_dim.11), calls=%async_computation | async-start | bytes 4194304 | tf_op jit(solution)/shard_map/all_to_all | solution.py:168
  45.5 4.9 %collective-permute-start = (bf16[128,1024]{1,0:T(8,128)(2,1)S(1)}, bf16[128,1024]{1,0:T(8,128)(2,1)S(1)}, u32[]{:S(2)}, u32[]{:S(2)}) collective-permute-start(bf16[128,1024]{1,0:T(8,128)(2,1)S(1)} %bitcast.19), channel_id=1, source_target_pairs={{0,60},{1,61},{2,62},{3,63},{4,8},{5,9},{6,10},{7,11},{8,4},{9,5},... | collective-permute-start | bytes 786440 | tf_op jit(solution)/shard_map/ppermute | solution.py:234
  50.4 3.7 %collective-permute-done = bf16[128,1024]{1,0:T(8,128)(2,1)S(1)} collective-permute-done((bf16[128,1024]{1,0:T(8,128)(2,1)S(1)}, bf16[128,1024]{1,0:T(8,128)(2,1)S(1)}, u32[]{:S(2)}, u32[]{:S(2)}) %collective-permute-start) | collective-permute-done | bytes 262176 | tf_op jit(solution)/shard_map/ppermute | solution.py:234
  54.1 0.9 pad_maximum_fusion.refs_0_
  55.0 3.1 %collective-permute-start.3 = (bf16[256,1024]{1,0:T(8,128)(2,1)}, bf16[256,1024]{1,0:T(8,128)(2,1)}, u32[]{:S(2)}, u32[]{:S(2)}) collective-permute-start(bf16[256,1024]{1,0:T(8,128)(2,1)} %pad_maximum_fusion.refs_0_), channel_id=1, source_target_pairs={{0,1},{1,2},{2,3},{3,0},{4,5},{5,6},{6,7},{7,4},{8,9},{9,10},{10,1... | collective-permute-start | bytes 1572872 | tf_op jit(solution)/shard_map/ppermute | solution.py:237
  58.1 3.4 %collective-permute-start.4 = (bf16[256,1024]{1,0:T(8,128)(2,1)}, bf16[256,1024]{1,0:T(8,128)(2,1)}, u32[]{:S(2)}, u32[]{:S(2)}) collective-permute-start(bf16[256,1024]{1,0:T(8,128)(2,1)} %pad_maximum_fusion.refs_0_), channel_id=1, source_target_pairs={{0,3},{1,0},{2,1},{3,2},{4,7},{5,4},{6,5},{7,6},{8,11},{9,8},{10,9... | collective-permute-start | bytes 1572872 | tf_op jit(solution)/shard_map/ppermute | solution.py:238
  61.5 0.0 copy-start
  61.5 4.8 %shard_map.73 = (bf16[128,1024]{1,0:T(8,128)(2,1)}, f32[128,512]{1,0:T(8,128)}) custom-call(bf16[1024,2048]{1,0:T(8,128)(2,1)} %bitcast.14, bf16[128,1024]{1,0:T(8,128)(2,1)} %bitcast.16, s32[17,128]{1,0:T(8,128)} %users_ref.1), custom_call_target="tpu_custom_call" | custom-call | tf_op jit(solution)/shard_map/pallas_call | solution.py:181
  66.4 4.4 %all-to-all-done = bf16[8,128,1024]{2,1,0:T(8,128)(2,1)S(1)} async-done(((bf16[8,128,1024]{2,1,0:T(8,128)(2,1)}), bf16[8,128,1024]{2,1,0:T(8,128)(2,1)S(1)}, u32[]{:S(2)}, u32[]{:S(2)}) %all-to-all-start) | async-done | bytes 2097184 | tf_op jit(solution)/shard_map/all_to_all | solution.py:168
  70.8 2.6 %shard_map.74.refs_7_ = bf16[128,1024]{1,0:T(8,128)(2,1)S(1)} custom-call(bf16[1024,1024]{1,0:T(8,128)(2,1)S(1)} %bitcast.9, bf16[512,1024]{1,0:T(8,128)(2,1)S(1)} %bitcast.10, bf16[128,1024]{1,0:T(8,128)(2,1)} %bitcast.17, bf16[128,1024]{1,0:T(8,128)(2,1)} %get-tuple-element.9.refs_3_, f32[128,512]{1,0:T(8,128)} %get-tuple-element.10.refs_4_, ...), custom_call_target="tpu_custom_call" | custom-call | tf_op jit(solution)/shard_map/pallas_call | solution.py:181
  73.4 7.2 %collective-permute-start.2 = (bf16[128,1024]{1,0:T(8,128)(2,1)S(1)}, bf16[128,1024]{1,0:T(8,128)(2,1)S(1)}, u32[]{:S(2)}, u32[]{:S(2)}) collective-permute-start(bf16[128,1024]{1,0:T(8,128)(2,1)S(1)} %shard_map.74.refs_7_), channel_id=1, source_target_pairs={{0,64},{64,128},{128,192},{192,256},{256,320},{320,384},{384,448},... | collective-permute-start | bytes 786440 | tf_op jit(solution)/shard_map/ppermute | solution.py:245
  80.6 1.0 slice.14
  81.6 3.6 %collective-permute-start.5 = (bf16[128,1024]{1,0:T(8,128)(2,1)S(1)}, bf16[128,1024]{1,0:T(8,128)(2,1)S(1)}, u32[]{:S(2)}, u32[]{:S(2)}) collective-permute-start(bf16[128,1024]{1,0:T(8,128)(2,1)S(1)} %bitcast.21), channel_id=1, source_target_pairs={{0,2},{1,3},{2,0},{3,1},{4,6},{5,7},{6,4},{7,5},{8,10},{9,11},{10,... | collective-permute-start | bytes 786440 | tf_op jit(solution)/shard_map/ppermute | solution.py:239
  85.1 3.2 %collective-permute-start.1 = (bf16[128,1024]{1,0:T(8,128)(2,1)}, bf16[128,1024]{1,0:T(8,128)(2,1)S(1)}, u32[]{:S(2)}, u32[]{:S(2)}) collective-permute-start(bf16[128,1024]{1,0:T(8,128)(2,1)} %copy-done.5), channel_id=1, source_target_pairs={{0,2},{1,3},{2,0},{3,1},{4,6},{5,7},{6,4},{7,5},{8,10},{9,11},{10,... | collective-permute-start | bytes 786440 | tf_op jit(solution)/shard_map/ppermute | solution.py:240
  88.4 0.2 shard_map.76.refs_6_
  88.6 4.1 %shard_map.75 = (bf16[128,1024]{1,0:T(8,128)(2,1)S(1)}, f32[128,512]{1,0:T(8,128)S(1)}) custom-call(bf16[128,1024]{1,0:T(8,128)(2,1)S(1)} %collective-permute-done.2.refs_0_.refs_2_, bf16[1024,2048]{1,0:T(8,128)(2,1)} %bitcast.15, bf16[128,1024]{1,0:T(8,128)(2,1)} %refs_5_.3, s32[17,128]{1,0:T(8,128)} %users_ref.1), custom_call_target="tpu_custom_call" | custom-call | tf_op jit(solution)/shard_map/pallas_call | solution.py:181
  92.7 0.0 copy-start.1
  92.7 0.6 collective-permute-done.5.refs_3_
  93.3 2.7 %shard_map.77.refs_4_ = f32[128,512]{1,0:T(8,128)S(1)} custom-call(bf16[256,1024]{1,0:T(8,128)(2,1)} %pad_maximum_fusion.refs_0_, bf16[256,1024]{1,0:T(8,128)(2,1)} %collective-permute-done.3.refs_1_, bf16[256,1024]{1,0:T(8,128)(2,1)} %collective-permute-done.4.refs_2_, bf16[128,1024]{1,0:T(8,128)(2,1)S(1)} %collective-permute-done.5.refs_3_, ...), custom_call_target="tpu_custom_call" | custom-call | tf_op jit(solution)/shard_map/pallas_call | solution.py:181
  96.0 1.3 %collective-permute-done.1.refs_0_ = bf16[128,1024]{1,0:T(8,128)(2,1)S(1)} collective-permute-done((bf16[128,1024]{1,0:T(8,128)(2,1)}, bf16[128,1024]{1,0:T(8,128)(2,1)S(1)}, u32[]{:S(2)}, u32[]{:S(2)}) %collective-permute-start.1) | collective-permute-done | bytes 262176 | tf_op jit(solution)/shard_map/ppermute | solution.py:240
  97.3 2.0 %shard_map.78 = bf16[2,128,1024]{2,1,0:T(8,128)(2,1)} custom-call(bf16[128,1024]{1,0:T(8,128)(2,1)S(1)} %collective-permute-done.1.refs_0_, bf16[512,1024]{1,0:T(8,128)(2,1)S(1)} %bitcast.11, bf16[128,1024]{1,0:T(8,128)(2,1)S(1)} %collective-permute-done.2.refs_0_.refs_2_, bf16[128,1024]{1,0:T(8,128)(2,1)S(1)} %get-tuple-element.11.refs_4_.refs_3_, ...), custom_call_target="tpu_custom_call" | custom-call | tf_op jit(solution)/shard_map/pallas_call | solution.py:181
  (13 shorter events, 0.1 us)
Async XLA Ops:
  37.1 0.8 copy-start.4
  39.5 31.2 %all-to-all-start = ((bf16[8,128,1024]{2,1,0:T(8,128)(2,1)}), bf16[8,128,1024]{2,1,0:T(8,128)(2,1)S(1)}, u32[]{:S(2)}, u32[]{:S(2)}) async-start(bf16[8,128,1024]{2,1,0:T(8,128)(2,1)} %broadcast_in_dim.11), calls=%async_computation | async-start | bytes 4194304 | tf_op jit(solution)/shard_map/all_to_all | solution.py:168
  45.5 8.6 %collective-permute-start = (bf16[128,1024]{1,0:T(8,128)(2,1)S(1)}, bf16[128,1024]{1,0:T(8,128)(2,1)S(1)}, u32[]{:S(2)}, u32[]{:S(2)}) collective-permute-start(bf16[128,1024]{1,0:T(8,128)(2,1)S(1)} %bitcast.19), channel_id=1, source_target_pairs={{0,60},{1,61},{2,62},{3,63},{4,8},{5,9},{6,10},{7,11},{8,4},{9,5},... | collective-permute-start | bytes 786440 | tf_op jit(solution)/shard_map/ppermute | solution.py:234
  54.1 7.4 %copy-start.5 = (bf16[128,1024]{1,0:T(8,128)(2,1)}, bf16[128,1024]{1,0:T(8,128)(2,1)S(1)}, u32[]{:S(2)}) copy-start(bf16[128,1024]{1,0:T(8,128)(2,1)S(1)} %collective-permute-done) | copy-start | bytes 786436
  55.0 38.3 %collective-permute-start.3 = (bf16[256,1024]{1,0:T(8,128)(2,1)}, bf16[256,1024]{1,0:T(8,128)(2,1)}, u32[]{:S(2)}, u32[]{:S(2)}) collective-permute-start(bf16[256,1024]{1,0:T(8,128)(2,1)} %pad_maximum_fusion.refs_0_), channel_id=1, source_target_pairs={{0,1},{1,2},{2,3},{3,0},{4,5},{5,6},{6,7},{7,4},{8,9},{9,10},{10,1... | collective-permute-start | bytes 1572872 | tf_op jit(solution)/shard_map/ppermute | solution.py:237
  58.1 35.2 %collective-permute-start.4 = (bf16[256,1024]{1,0:T(8,128)(2,1)}, bf16[256,1024]{1,0:T(8,128)(2,1)}, u32[]{:S(2)}, u32[]{:S(2)}) collective-permute-start(bf16[256,1024]{1,0:T(8,128)(2,1)} %pad_maximum_fusion.refs_0_), channel_id=1, source_target_pairs={{0,3},{1,0},{2,1},{3,2},{4,7},{5,4},{6,5},{7,6},{8,11},{9,8},{10,9... | collective-permute-start | bytes 1572872 | tf_op jit(solution)/shard_map/ppermute | solution.py:238
  61.5 9.3 %copy-start = (bf16[1,512,1024]{2,1,0:T(8,128)(2,1)S(1)}, bf16[1,512,1024]{2,1,0:T(8,128)(2,1)}, u32[]{:S(2)}) copy-start(bf16[1,512,1024]{2,1,0:T(8,128)(2,1)} %param.10) | copy-start | bytes 3145732
  70.8 17.6 %copy-start.2 = (s32[17,128]{1,0:T(8,128)S(1)}, s32[17,128]{1,0:T(8,128)}, u32[]{:S(2)}) copy-start(s32[17,128]{1,0:T(8,128)} %users_ref.1) | copy-start | bytes 26116
  70.8 17.6 %copy-start.3 = (s32[17,4]{0,1:T(4,128)S(1)}, s32[17,4]{0,1:T(4,128)}, u32[]{:S(2)}) copy-start(s32[17,4]{0,1:T(4,128)} %param.13) | copy-start | bytes 820
  73.4 15.2 %collective-permute-start.2 = (bf16[128,1024]{1,0:T(8,128)(2,1)S(1)}, bf16[128,1024]{1,0:T(8,128)(2,1)S(1)}, u32[]{:S(2)}, u32[]{:S(2)}) collective-permute-start(bf16[128,1024]{1,0:T(8,128)(2,1)S(1)} %shard_map.74.refs_7_), channel_id=1, source_target_pairs={{0,64},{64,128},{128,192},{192,256},{256,320},{320,384},{384,448},... | collective-permute-start | bytes 786440 | tf_op jit(solution)/shard_map/ppermute | solution.py:245
  81.6 11.7 %collective-permute-start.5 = (bf16[128,1024]{1,0:T(8,128)(2,1)S(1)}, bf16[128,1024]{1,0:T(8,128)(2,1)S(1)}, u32[]{:S(2)}, u32[]{:S(2)}) collective-permute-start(bf16[128,1024]{1,0:T(8,128)(2,1)S(1)} %bitcast.21), channel_id=1, source_target_pairs={{0,2},{1,3},{2,0},{3,1},{4,6},{5,7},{6,4},{7,5},{8,10},{9,11},{10,... | collective-permute-start | bytes 786440 | tf_op jit(solution)/shard_map/ppermute | solution.py:239
  85.1 12.2 %collective-permute-start.1 = (bf16[128,1024]{1,0:T(8,128)(2,1)}, bf16[128,1024]{1,0:T(8,128)(2,1)S(1)}, u32[]{:S(2)}, u32[]{:S(2)}) collective-permute-start(bf16[128,1024]{1,0:T(8,128)(2,1)} %copy-done.5), channel_id=1, source_target_pairs={{0,2},{1,3},{2,0},{3,1},{4,6},{5,7},{6,4},{7,5},{8,10},{9,11},{10,... | collective-permute-start | bytes 786440 | tf_op jit(solution)/shard_map/ppermute | solution.py:240
  92.7 4.6 %copy-start.1 = (bf16[128,1024]{1,0:T(8,128)(2,1)S(1)}, bf16[128,1024]{1,0:T(8,128)(2,1)}, u32[]{:S(2)}) copy-start(bf16[128,1024]{1,0:T(8,128)(2,1)} %refs_5_.3) | copy-start | bytes 786436
